TPU v7x, 32 devices: a whole 2x2x4 slice. The times are simulated.
32 devices in a mesh: gx: 4 (over y, x), gy: 8 (over z, core).
Axes of the slice: x: 2, y: 2, z: 4, core: 2. Of those that a mesh axis runs over, the one named last changes fastest.
Arguments:
- background: bfloat16 [40, 64, 256, 128], P(None, 'gx', 'gy'), may hold values from -6 to 6
- obs_perturb: bfloat16 [4, 8, 40, 256], P('gx', 'gy'), may hold values from -1.796875 to 1.796875
- innovation: float32 [4, 8, 256], P('gx', 'gy'), may hold values from -3.8 to 3.8
- obs_precision: float32 [4, 8, 256], P('gx', 'gy'), may hold values from 0.3 to 3
- obs_column: int32 [4, 8, 256], P('gx', 'gy'), may hold values from 0 to 511
- obs_count: int32 [4, 8], P('gx', 'gy'), may hold values from 64 to 256, as said below
Outputs:
- analysis: bfloat16 [40, 64, 256, 128], P(None, 'gx', 'gy')
Inputs may be any that keep to these rules, and one draw needn't show every extreme that they name: Slots 0 to obs_count - 1 of a tile hold observations, the others are padding; in every draw some tile has all 256 slots live.
All inputs are finite; a program needn't handle non-finite values.
Results may differ from a plain program's by a relative error of at most 0.001.
Values sent between devices are 32-bit elements; how exact they have to be, the bound alone decides.
No kernel may reach another device: no remote copies, remote signals or barrier semaphores. Data moves between devices by JAX's collectives and lax.ppermute only.
A program may use at most 128 MiB of HBM per device.

v0:
```python
import math

import jax
import jax.numpy as jnp
from jax import lax
from jax.sharding import PartitionSpec as P

SPAN = 2


def with_halo(cells, sides, width):
    for axis, dim in sides:
        count = lax.axis_size(axis)
        head = lax.slice_in_dim(cells, 0, width, axis=dim)
        tail = lax.slice_in_dim(cells, cells.shape[dim] - width, cells.shape[dim], axis=dim)
        cells = jnp.concatenate(
            [
                lax.ppermute(tail, axis, [(i, (i + 1) % count) for i in range(count)]),
                cells,
                lax.ppermute(head, axis, [((i + 1) % count, i) for i in range(count)]),
            ],
            axis=dim,
        )
    return cells


def pair_table(centered, values):
    members = centered.shape[0]
    squares = (centered[:, None, :] * centered[None, :, :]).reshape(
        members * members, centered.shape[1]
    )
    return jnp.concatenate([squares, centered * values[None, :]], axis=0)


def taper(east_pos, north_pos, centre_east, centre_north, period, radius):
    offset_east = (
        jnp.mod(east_pos[:, None] - centre_east[None, :] + 0.5 * period, period) - 0.5 * period
    )
    offset_north = north_pos[:, None] - centre_north[None, :]
    ratio = (offset_east * offset_east + offset_north * offset_north) / (radius * radius)
    return jnp.square(jnp.maximum(1.0 - ratio, 0.0))


def region_centres(
    tile_east, northward_tile, count_east, count_north, span, width_east, width_north
):
    rows_east = (jnp.arange(count_east) * span).astype(jnp.float32) + 0.5 * span
    rows_north = (jnp.arange(count_north) * span).astype(jnp.float32) + 0.5 * span
    base_east = (tile_east * width_east).astype(jnp.float32)
    base_north = (northward_tile * width_north).astype(jnp.float32)
    centre_east = jnp.broadcast_to(
        base_east + rows_east[:, None], (count_east, count_north)
    ).reshape(-1)
    centre_north = jnp.broadcast_to(
        base_north + rows_north[None, :], (count_east, count_north)
    ).reshape(-1)
    return (centre_east, centre_north)


def chol_lower(system):
    members = system.shape[0]
    rows = jnp.arange(members)
    remain = system
    columns = []
    for pivot_id in range(members):
        pivot = jnp.sqrt(remain[pivot_id, pivot_id])
        column = jnp.where((rows >= pivot_id)[:, None], remain[:, pivot_id] / pivot[None, :], 0.0)
        columns.append(column)
        remain = remain - column[:, None, :] * column[None, :, :]
    return jnp.stack(columns, axis=1)


def lower_inverse(factor):
    members = factor.shape[0]
    remain = jnp.broadcast_to(jnp.eye(members, dtype=factor.dtype)[:, :, None], factor.shape)
    solved = []
    for pivot_id in range(members):
        row_now = remain[pivot_id] / factor[pivot_id, pivot_id][None, :]
        solved.append(row_now)
        remain = remain - factor[:, pivot_id][:, None, :] * row_now[None, :, :]
    return jnp.stack(solved, axis=0)


def transform_of(gram, prior_term, members):
    square = members * members
    system = (
        gram[:square].reshape(members, members, -1)
        + prior_term * jnp.eye(members, dtype=gram.dtype)[:, :, None]
    )
    pull = gram[square:]
    inverse = lower_inverse(chol_lower(system))
    inner = jnp.einsum("imr,mr->ir", inverse, pull, precision=lax.Precision.HIGHEST)
    mean_weights = jnp.einsum("imr,ir->mr", inverse, inner, precision=lax.Precision.HIGHEST)
    return mean_weights[:, None, :] + math.sqrt(members - 1) * jnp.transpose(inverse, (1, 0, 2))


def interp_matrix(columns, regions, span):
    position = jnp.arange(columns).astype(jnp.float32) + 0.5
    centre = (jnp.arange(regions + 2) - 1).astype(jnp.float32) * span + 0.5 * span
    return jnp.maximum(1.0 - jnp.abs(position[:, None] - centre[None, :]) / span, 0.0)


def apply_tile(state_tile, local_frame, span):
    members, cols_east, cols_north, levels = state_tile.shape
    interpolation_rows = interp_matrix(cols_east, local_frame.shape[0] - 2, span)
    interp_cols = interp_matrix(cols_north, local_frame.shape[1] - 2, span)
    halfway_result = jnp.einsum(
        "br,rjg->bjg", interpolation_rows, local_frame, precision=lax.Precision.HIGHEST
    )
    column_transform = jnp.einsum(
        "bq,aqm->abm", interp_cols, halfway_result, precision=lax.Precision.HIGHEST
    )
    column_transform = column_transform.reshape(cols_east, cols_north, members, members)
    float_state = state_tile.astype(jnp.float32)
    centre_mean = jnp.mean(float_state, axis=0)
    spread = float_state - centre_mean[None]
    update = jnp.einsum(
        "jabl,abjk->kabl", spread, column_transform, precision=lax.Precision.HIGHEST
    )
    return (centre_mean[None] + update).astype(jnp.bfloat16)


def per_device(background, obs_perturb, innovation, obs_precision, obs_column, obs_count):
    members, cols_east, cols_north, levels = background.shape
    square = members * members
    regions_east = cols_east // SPAN
    regions_north = cols_north // SPAN
    count_east = lax.axis_size("gx")
    count_north = lax.axis_size("gy")
    tile_east = lax.axis_index("gx")
    northward_tile = lax.axis_index("gy")
    slot_count = obs_perturb.shape[3]
    centered = obs_perturb[0, 0].astype(jnp.float32)
    centered = centered - jnp.mean(centered, axis=0, keepdims=True)
    values = innovation[0, 0]
    slots = jnp.arange(slot_count, dtype=jnp.int32)
    weight = obs_precision[0, 0] * (slots < obs_count[0, 0]).astype(jnp.float32)
    column = obs_column[0, 0]
    east_pos = (tile_east * cols_east + column // cols_north).astype(jnp.float32) + 0.5
    north_pos = (northward_tile * cols_north + column % cols_north).astype(jnp.float32) + 0.5
    numer, denom = lax.psum(
        (
            jnp.sum(weight * values * values),
            jnp.sum(weight * jnp.sum(centered * centered, axis=0)) / (members - 1),
        ),
        ("gx", "gy"),
    )
    prior_term = (members - 1) / (numer / denom)
    period = float(count_east * cols_east)
    radius = float(cols_east)
    bundle = jnp.concatenate(
        [centered, values[None], weight[None], east_pos[None], north_pos[None]], axis=0
    )
    nearby = with_halo(bundle[None, None], (("gx", 0), ("gy", 1)), 1)
    centre_east, centre_north = region_centres(
        tile_east, northward_tile, regions_east, regions_north, SPAN, cols_east, cols_north
    )
    gram = jnp.zeros((square + members, regions_east * regions_north), jnp.float32)
    for place_east in range(3):
        for place_north in range(3):
            block_obs = nearby[place_east, place_north]
            products = pair_table(block_obs[:members], block_obs[members])
            reach = taper(
                block_obs[members + 2],
                block_obs[members + 3],
                centre_east,
                centre_north,
                period,
                radius,
            )
            reach = reach * block_obs[members + 1][:, None]
            gram = gram + jnp.dot(
                products, reach, precision=lax.Precision.HIGHEST, preferred_element_type=jnp.float32
            )
    trans = transform_of(gram, prior_term, members)
    grid = jnp.transpose(trans, (2, 0, 1)).reshape(regions_east, regions_north, square)
    rims = with_halo(grid, (("gx", 0), ("gy", 1)), 1)
    first_row = jnp.where(northward_tile == 0, rims[:, 1:2], rims[:, 0:1])
    last_row = jnp.where(northward_tile == count_north - 1, rims[:, -2:-1], rims[:, -1:])
    local_frame = jnp.concatenate([first_row, rims[:, 1:-1], last_row], axis=1)
    return apply_tile(background, local_frame, float(SPAN))


def solution(mesh):
    return jax.shard_map(
        per_device,
        mesh=mesh,
        in_specs=(
            P(None, "gx", "gy", None),
            P("gx", "gy", None, None),
            P("gx", "gy", None),
            P("gx", "gy", None),
            P("gx", "gy", None),
            P("gx", "gy"),
        ),
        out_specs=P(None, "gx", "gy", None),
        check_vma=False,
    )
```

profile of v0, /device:TPU:0, one launch (start us, length us, event | category | flops | bytes accessed | tf_op | source)
XLA Modules:
  0.0 173.7 jit_solution(7164807621013739276)
XLA Ops:
  4.3 4.0 %collective-permute-start.1 = (f32[1,1,44,256]{3,2,1,0:T(8,128)S(1)}, f32[1,1,44,256]{3,2,1,0:T(8,128)S(1)}, u32[]{:S(2)}, u32[]{:S(2)}) collective-permute-start(f32[1,1,44,256]{3,2,1,0:T(8,128)S(1)} %bitcast.666), channel_id=1, source_target_pairs={{8,0},{16,8},{24,16},{0,24},{9,1},{17,9},{25,17},{1,25},{10,2},{18... | collective-permute-start | bytes 135176 | tf_op jit(solution)/shard_map/ppermute | solution.py:20
  10.3 41.2 %all-reduce = (f32[]{:T(128)}, f32[]{:T(128)}) all-reduce(f32[]{:T(128)S(6)} %div.1223, f32[]{:T(128)} %get-tuple-element.5), channel_id=1, replica_groups=mesh['gx'=4,'gy'=8] {'gx','gy'}, use_global_device_ids=true, to_apply=%region_4.5 | all-reduce | flops 2 | bytes 16 | tf_op jit(solution)/shard_map/psum | solution.py:141
  52.9 3.4 %convert_reduce_fusion = f32[16,32,128]{2,1,0:T(8,128)S(1)} fusion(bf16[40,16,32,128]{3,2,1,0:T(8,128)(2,1)} %param.6), kind=kLoop, calls=%fused_computation.1 | loop fusion | flops 5177344 | bytes 5505024 | tf_op jit(solution)/shard_map/reduce_sum | solution.py:115
  56.9 5.5 %convert_subtract_fusion = f32[40,16,32,128]{3,2,1,0:T(8,128)} fusion(bf16[40,16,32,128]{3,2,1,0:T(8,128)(2,1)S(1)} %copy-done, f32[16,32,128]{2,1,0:T(8,128)S(1)} %broadcast_multiply_fusion.9), kind=kLoop, calls=%fused_computation | loop fusion | flops 5242880 | bytes 15990784 | tf_op jit(solution)/shard_map/sub | solution.py:116
  63.3 1.1 collective-permute-start.3
  65.2 1.7 fusion.19
  66.9 4.4 %collective-permute-done.2 = f32[3,1,44,256]{3,2,1,0:T(8,128)S(1)} collective-permute-done((f32[3,1,44,256]{3,2,1,0:T(8,128)S(1)}, f32[3,1,44,256]{3,2,1,0:T(8,128)S(1)}, u32[]{:S(2)}, u32[]{:S(2)}) %collective-permute-start.2) | collective-permute-done | bytes 135200 | tf_op jit(solution)/shard_map/ppermute | solution.py:18
  72.1 1.7 convolution_add_fusion.7
  73.8 1.7 convolution_add_fusion.6
  75.4 1.7 convolution_add_fusion.5
  77.1 1.7 convolution_add_fusion.4
  78.8 1.7 convolution_add_fusion.3
  80.4 1.9 %convolution_add_fusion.2 = f32[1640,128]{1,0:T(8,128)S(1)} fusion(f32[1640,128]{1,0:T(8,128)S(1)} %convolution_add_fusion.3, f32[40,256]{1,0:T(8,128)S(1)} %get-tuple-element.49, f32[1600,256]{1,0:T(8,128)S(1)} %bitcast.608, f32[256]{0:T(256)S(1)} %bitcast.733, f32[256]{0:T(256)S(1)} %bitcast.734, f32[256]{0:T(256)S(1)} %bitcast.732, f32[128]{0:T(128)S(1)} %sub.617, ...), kind=kOutput, calls=%fused_computation.10 | convolution fusion | flops 646093824 | bytes 3362816 | tf_op jit(solution)/shard_map/dot_general | solution.py:172
  82.3 1.7 convolution_add_fusion.1
  84.0 1.7 convolution_add_fusion
  88.2 0.8 multiply_subtract_fusion.68
  89.3 0.8 multiply_subtract_fusion.66
  94.6 0.9 multiply_subtract_fusion.54
  109.1 0.9 slice.950
  110.1 1.4 collective-permute-start.4
  111.8 0.9 slice.952
  112.7 1.5 collective-permute-start.5
  114.2 1.2 copy.138
  115.5 1.7 reshape.2960
  117.1 1.4 copy.140
  119.4 5.9 %collective-permute-done.6 = f32[10,1,1600]{2,0,1:T(8,128)S(1)} collective-permute-done((f32[10,1,1600]{2,0,1:T(8,128)S(1)}, f32[10,1,1600]{2,0,1:T(8,128)S(1)}, u32[]{:S(2)}, u32[]{:S(2)}) %collective-permute-start.6) | collective-permute-done | bytes 64032 | tf_op jit(solution)/shard_map/ppermute | solution.py:18
  126.3 2.3 %collective-permute-done.7 = f32[10,1,1600]{2,0,1:T(8,128)S(1)} collective-permute-done((f32[10,1,1600]{2,0,1:T(8,128)S(1)}, f32[10,1,1600]{2,0,1:T(8,128)S(1)}, u32[]{:S(2)}, u32[]{:S(2)}) %collective-permute-start.7) | collective-permute-done | bytes 64032 | tf_op jit(solution)/shard_map/ppermute | solution.py:20
  128.6 2.8 %fusion.6 = f32[16,18,1600]{2,0,1:T(8,128)S(1)} fusion(f32[10,1,1600]{2,0,1:T(8,128)S(1)} %broadcast_select_fusion, f32[1,16,1600]{2,0,1:T(1,128)} %collective-permute-done.5, f32[8,16,1600]{2,0,1:T(8,128)S(1)} %copy.140, f32[1,16,1600]{2,0,1:T(1,128)S(1)} %collective-permute-done.4, f32[10,1,1600]{2,0,1:T(8,128)S(1)} %get-tuple-element.9, ...), kind=kOutput, calls=%fused_computation.16 | convolution fusion | flops 56448800 | bytes 2995304 | tf_op jit(solution)/shard_map/br,rjg->bjg/dot_general | solution.py:107
  131.4 3.4 %convolution_bitcast_fusion = f32[16,32,1600]{2,1,0:T(8,128)S(1)} fusion(f32[16,18,1600]{2,0,1:T(8,128)S(1)} %fusion.6, f32[18]{0:T(128)S(1)} %multiply_add_fusion, f32[32]{0:T(128)S(1)} %convert_add_fusion.3), kind=kOutput, calls=%fused_computation.6 | convolution fusion | flops 176950080 | bytes 5120200 | tf_op jit(solution)/shard_map/bq,aqm->abm/dot_general | solution.py:110
  134.8 6.2 %reshape.2961 = f32[16,32,40,40]{3,2,1,0:T(8,128)} reshape(f32[16,32,1600]{2,1,0:T(8,128)S(1)} %convolution_bitcast_fusion) | data formatting | bytes 6553600 | tf_op jit(solution)/shard_map/reshape | solution.py:113
  141.0 28.6 %fusion.2 = bf16[40,16,32,128]{3,0,2,1:T(8,128)(2,1)S(1)} fusion(f32[16,32,128]{2,1,0:T(8,128)} %copy-done.1, f32[16,32,40,40]{3,2,1,0:T(8,128)} %reshape.2961, f32[40,16,32,128]{3,2,1,0:T(8,128)} %convert_subtract_fusion), kind=kOutput, calls=%fused_computation.5 | convolution fusion | flops 1263534080 | bytes 19267584 | tf_op jit(solution)/shard_map/jabl,abjk->kabl/dot_general | solution.py:117
  169.6 3.6 %copy.144 = bf16[40,16,32,128]{3,2,1,0:T(8,128)(2,1)} copy(bf16[40,16,32,128]{3,0,2,1:T(8,128)(2,1)S(1)} %fusion.2) | data formatting | bytes 10485760 | tf_op jit(solution)/shard_map/convert_element_type | solution.py:120
  (390 shorter events, 29.3 us)
Async XLA Ops:
  0.0 8.9 %copy-start.3 = (f32[1,1,256]{2,1,0:T(1,128)S(1)}, f32[1,1,256]{2,1,0:T(1,128)}, u32[]{:S(2)}) copy-start(f32[1,1,256]{2,1,0:T(1,128)} %param.9) | copy-start | bytes 3076
  0.0 8.9 %copy-start.2 = (f32[1,1,256]{2,1,0:T(1,128)S(1)}, f32[1,1,256]{2,1,0:T(1,128)}, u32[]{:S(2)}) copy-start(f32[1,1,256]{2,1,0:T(1,128)} %param.8) | copy-start | bytes 3076
  0.0 8.9 %copy-start.4 = (s32[1,1,256]{2,1,0:T(1,128)S(1)}, s32[1,1,256]{2,1,0:T(1,128)}, u32[]{:S(2)}) copy-start(s32[1,1,256]{2,1,0:T(1,128)} %param.10) | copy-start | bytes 3076
  4.3 59.0 %collective-permute-start.1 = (f32[1,1,44,256]{3,2,1,0:T(8,128)S(1)}, f32[1,1,44,256]{3,2,1,0:T(8,128)S(1)}, u32[]{:S(2)}, u32[]{:S(2)}) collective-permute-start(f32[1,1,44,256]{3,2,1,0:T(8,128)S(1)} %bitcast.666), channel_id=1, source_target_pairs={{8,0},{16,8},{24,16},{0,24},{9,1},{17,9},{25,17},{1,25},{10,2},{18... | collective-permute-start | bytes 135176 | tf_op jit(solution)/shard_map/ppermute | solution.py:20
  8.3 55.0 %collective-permute-start = (f32[1,1,44,256]{3,2,1,0:T(8,128)S(1)}, f32[1,1,44,256]{3,2,1,0:T(8,128)S(1)}, u32[]{:S(2)}, u32[]{:S(2)}) collective-permute-start(f32[1,1,44,256]{3,2,1,0:T(8,128)S(1)} %bitcast.667), channel_id=1, source_target_pairs={{0,8},{8,16},{16,24},{24,0},{1,9},{9,17},{17,25},{25,1},{2,10},{10... | collective-permute-start | bytes 135176 | tf_op jit(solution)/shard_map/ppermute | solution.py:18
  52.9 4.0 %copy-start = (bf16[40,16,32,128]{3,2,1,0:T(8,128)(2,1)S(1)}, bf16[40,16,32,128]{3,2,1,0:T(8,128)(2,1)}, u32[]{:S(2)}) copy-start(bf16[40,16,32,128]{3,2,1,0:T(8,128)(2,1)} %param.6) | copy-start | bytes 15728644
  56.9 5.5 %copy-start.1 = (f32[16,32,128]{2,1,0:T(8,128)}, f32[16,32,128]{2,1,0:T(8,128)S(1)}, u32[]{:S(2)}) copy-start(f32[16,32,128]{2,1,0:T(8,128)S(1)} %broadcast_multiply_fusion.9) | copy-start | bytes 786436
  63.3 8.1 %collective-permute-start.3 = (f32[3,1,44,256]{3,2,1,0:T(8,128)S(1)}, f32[3,1,44,256]{3,2,1,0:T(8,128)S(1)}, u32[]{:S(2)}, u32[]{:S(2)}) collective-permute-start(f32[3,1,44,256]{3,2,1,0:T(8,128)S(1)} %pad_maximum_fusion), channel_id=1, source_target_pairs={{1,0},{2,1},{3,2},{4,3},{5,4},{6,5},{7,6},{0,7},{9,8},{10,9},{11,1... | collective-permute-start | bytes 405512 | tf_op jit(solution)/shard_map/ppermute | solution.py:20
  64.4 6.8 %collective-permute-start.2 = (f32[3,1,44,256]{3,2,1,0:T(8,128)S(1)}, f32[3,1,44,256]{3,2,1,0:T(8,128)S(1)}, u32[]{:S(2)}, u32[]{:S(2)}) collective-permute-start(f32[3,1,44,256]{3,2,1,0:T(8,128)S(1)} %pad_maximum_fusion), channel_id=1, source_target_pairs={{0,1},{1,2},{2,3},{3,4},{4,5},{5,6},{6,7},{7,0},{8,9},{9,10},{10,1... | collective-permute-start | bytes 405512 | tf_op jit(solution)/shard_map/ppermute | solution.py:18
  110.1 8.5 %collective-permute-start.4 = (f32[1,16,1600]{2,0,1:T(1,128)}, f32[1,16,1600]{2,0,1:T(1,128)S(1)}, u32[]{:S(2)}, u32[]{:S(2)}) collective-permute-start(f32[1,16,1600]{2,0,1:T(1,128)} %slice.950), channel_id=1, source_target_pairs={{0,8},{8,16},{16,24},{24,0},{1,9},{9,17},{17,25},{25,1},{2,10},{10... | collective-permute-start | bytes 307208 | tf_op jit(solution)/shard_map/ppermute | solution.py:18
  112.7 5.9 %collective-permute-start.5 = (f32[1,16,1600]{2,0,1:T(1,128)}, f32[1,16,1600]{2,0,1:T(1,128)}, u32[]{:S(2)}, u32[]{:S(2)}) collective-permute-start(f32[1,16,1600]{2,0,1:T(1,128)} %slice.952), channel_id=1, source_target_pairs={{8,0},{16,8},{24,16},{0,24},{9,1},{17,9},{25,17},{1,25},{10,2},{18... | collective-permute-start | bytes 307208 | tf_op jit(solution)/shard_map/ppermute | solution.py:20
  119.3 6.0 %collective-permute-start.6 = (f32[10,1,1600]{2,0,1:T(8,128)S(1)}, f32[10,1,1600]{2,0,1:T(8,128)S(1)}, u32[]{:S(2)}, u32[]{:S(2)}) collective-permute-start(f32[10,1,1600]{2,0,1:T(8,128)S(1)} %pad_maximum_fusion.1), channel_id=1, source_target_pairs={{0,1},{1,2},{2,3},{3,4},{4,5},{5,6},{6,7},{7,0},{8,9},{9,10},{10,1... | collective-permute-start | bytes 192008 | tf_op jit(solution)/shard_map/ppermute | solution.py:18
  126.0 2.6 %collective-permute-start.7 = (f32[10,1,1600]{2,0,1:T(8,128)S(1)}, f32[10,1,1600]{2,0,1:T(8,128)S(1)}, u32[]{:S(2)}, u32[]{:S(2)}) collective-permute-start(f32[10,1,1600]{2,0,1:T(8,128)S(1)} %get-tuple-element.10), channel_id=1, source_target_pairs={{1,0},{2,1},{3,2},{4,3},{5,4},{6,5},{7,6},{0,7},{9,8},{10,9},{11,1... | collective-permute-start | bytes 192008 | tf_op jit(solution)/shard_map/ppermute | solution.py:20
where the time goes:
time: 177 us; the launch traced here: 174 us
  matrix products  49.9 us (28%)
  blocking collectives  41.2 us (23%)
  other arithmetic  36.2 us (20%)
  local copies, waits for them, and re-layouts  19.8 us (11%)
  waiting for transfers between devices  12.6 us (7%)
  starting transfers between devices  8.84 us (5%)
  between operations  5.19 us (3%)
    psum x1, blocking collectives, per_device(): lax.psum((jnp.sum(weight * values * values), jnp.sum(weight * jnp.sum(cen...  41.2 us
    dot_general x1, matrix products, apply_tile(): jnp.einsum('jabl,abjk->kabl', spread, column_transform, precision=lax.Pre...  28.6 us
    dot_general x9, matrix products, per_device(): jnp.dot(products, reach, precision=lax.Precision.HIGHEST, preferred_eleme...  15.1 us
    sub x39, other arithmetic, chol_lower(): remain = remain - column[:, None, :] * column[None, :, :]  11.8 us
    ppermute x4, waiting for transfers between devices, with_halo(): lax.ppermute(tail, axis, [(i, (i + 1) % count) for i in range(count)])  10.3 us
    ppermute x4, starting transfers between devices, with_halo(): lax.ppermute(head, axis, [((i + 1) % count, i) for i in range(count)])  6.91 us
    reshape x1, local copies, waits for them, and re-layouts, apply_tile(): column_transform.reshape(cols_east, cols_north, members, members)  6.18 us
    sub x1, other arithmetic, apply_tile(): spread = float_state - centre_mean[None]  5.52 us
  transfers between devices with their start and end apart: 8, of which 3 were waited for; matrix products, arithmetic and copies ran while one was open for 11% of the time, Pallas kernels for 0%

commit v1 on v0

v1 whole, which is shorter than its diff:
```python
import functools
import math

import jax
import jax.numpy as jnp
from jax import lax
from jax.experimental import pallas as pl
from jax.experimental.pallas import tpu as pltpu
from jax.sharding import PartitionSpec as P

SPAN = 2
LANES = 128
SUB = 8
ROWS = 48
F32 = jnp.float32
BF16 = jnp.bfloat16


def pair_rows(members):
    offsets, total = [], 0
    for i in range(members):
        offsets.append(total)
        total += members - (i // SUB) * SUB
    pull = total
    total += members
    return offsets, pull, -(-total // 16) * 16


def prep_kernel(cols_east, cols_north, count_ref, perturb_ref, innov_ref, prec_ref, column_ref, out_ref):
    members, slots = perturb_ref.shape
    tile_east, tile_north = lax.axis_index("gx"), lax.axis_index("gy")
    spread = perturb_ref[...].astype(F32)
    spread = spread - jnp.sum(spread, axis=0, keepdims=True) / members
    lane = lax.broadcasted_iota(jnp.int32, (1, slots), 1)
    weight = jnp.where(lane < count_ref[0, 0], prec_ref[...], 0.0)
    root = jnp.sqrt(weight)
    values = innov_ref[...]
    column = column_ref[...]
    east = lax.div(column, cols_north)
    north = column - east * cols_north
    east = (tile_east * cols_east + east).astype(F32) + 0.5
    north = (tile_north * cols_north + north).astype(F32) + 0.5
    numer = jnp.sum(weight * values * values, axis=1, keepdims=True)
    variance = jnp.sum(spread * spread, axis=0, keepdims=True)
    denom = jnp.sum(weight * variance, axis=1, keepdims=True) / (members - 1)
    out_ref[0:members, :] = spread * root
    row = lax.broadcasted_iota(jnp.int32, (ROWS - members, slots), 0)
    rest = jnp.zeros((ROWS - members, slots), F32)
    for place, value in enumerate((values * root, east, north, numer, denom)):
        rest = jnp.where(row == place, value, rest)
    out_ref[members:ROWS, :] = rest


def gram_kernel(members, cols_east, cols_north, obs_ref, out_ref, lhs_hi, lhs_lo, rhs_hi, rhs_lo):
    tiles = obs_ref.shape[0] // ROWS
    slots = obs_ref.shape[1]
    offsets, pull_row, total = pair_rows(members)
    regions_north = cols_north // SPAN
    deep = regions_north // 2 + 2
    lanes = 2 * LANES
    tile_east, tile_north = lax.axis_index("gx"), lax.axis_index("gy")
    count_north = lax.axis_size("gy")
    lane = lax.broadcasted_iota(jnp.int32, (1, lanes), 1)
    half = (lane >= LANES).astype(jnp.int32)
    inner = (lane - half * LANES).astype(F32)
    place_east = jnp.floor((inner + 0.5) / deep)
    place_north = inner - place_east * deep
    centre_east = (tile_east * cols_east).astype(F32) + (place_east - 1.0) * SPAN + 0.5 * SPAN
    place_north = place_north + (tile_north * regions_north + half * (regions_north // 2) - 1).astype(F32)
    place_north = jnp.clip(place_north, 0.0, float(count_north * regions_north - 1))
    centre_north = place_north * SPAN + 0.5 * SPAN
    period = float(lax.axis_size("gx") * cols_east)
    radius = float(cols_east)
    for t in range(tiles):
        base = t * ROWS
        place = jnp.transpose(obs_ref[base + members : base + ROWS, :])
        east, north = place[:, 1:2], place[:, 2:3]
        ahead = east - centre_east + 0.5 * period
        away = ahead - period * jnp.floor(ahead * (1.0 / period)) - 0.5 * period
        up = north - centre_north
        near = jnp.maximum(1.0 - (away * away + up * up) * (1.0 / (radius * radius)), 0.0)
        taper = near * near
        hi = taper.astype(BF16)
        rhs_hi[t * slots : (t + 1) * slots, :] = hi
        rhs_lo[t * slots : (t + 1) * slots, :] = (taper - hi.astype(F32)).astype(BF16)
        span = slice(t * slots, (t + 1) * slots)
        for i in range(0, members, 2):
            first = (i // SUB) * SUB
            rows = obs_ref[base + first : base + members, :]
            table = jnp.concatenate(
                [obs_ref[base + i : base + i + 1, :] * rows, obs_ref[base + i + 1 : base + i + 2, :] * rows], axis=0
            )
            hi = table.astype(BF16)
            lhs_hi[offsets[i] : offsets[i] + table.shape[0], span] = hi
            lhs_lo[offsets[i] : offsets[i] + table.shape[0], span] = (table - hi.astype(F32)).astype(BF16)
        table = obs_ref[base + members : base + members + 1, :] * obs_ref[base : base + members, :]
        table = jnp.concatenate([table, jnp.zeros((total - pull_row - members, slots), F32)], axis=0)
        hi = table.astype(BF16)
        lhs_hi[pull_row:total, span] = hi
        lhs_lo[pull_row:total, span] = (table - hi.astype(F32)).astype(BF16)
    left = jnp.concatenate([lhs_hi[...], lhs_lo[...], lhs_hi[...]], axis=1)
    right = jnp.concatenate([rhs_hi[...], rhs_hi[...], rhs_lo[...]], axis=0)
    out_ref[...] = jnp.dot(left, right, preferred_element_type=F32)


def gram_table(bundles, members, cols_east, cols_north):
    total = pair_rows(members)[2]
    deep = bundles.shape[0] // ROWS * bundles.shape[1]
    return pl.pallas_call(
        functools.partial(gram_kernel, members, cols_east, cols_north),
        out_shape=jax.ShapeDtypeStruct((total, 2 * LANES), F32),
        in_specs=[pl.BlockSpec(memory_space=pltpu.VMEM)],
        out_specs=pl.BlockSpec(memory_space=pltpu.VMEM),
        scratch_shapes=[
            pltpu.VMEM((total, deep), BF16),
            pltpu.VMEM((total, deep), BF16),
            pltpu.VMEM((deep, 2 * LANES), BF16),
            pltpu.VMEM((deep, 2 * LANES), BF16),
        ],
        compiler_params=pltpu.CompilerParams(vmem_limit_bytes=24 << 20),
        cost_estimate=pl.CostEstimate(flops=6 * total * deep * 2 * LANES, bytes_accessed=1 << 21, transcendentals=0),
        name="gram_table",
    )(bundles)


def analysis_kernel(
    members, grams, sums_a, sums_b, state_ref, out_ref, u_ref, v_ref, t_ref, s_ref, w_ref, b_ref, o_ref,
    state_v, out_v, in_sem, out_sem,
):
    _, cols_east, cols_north, levels = state_v.shape
    offsets, pull_row, _ = pair_rows(members)
    wide = 2 * LANES
    blocks = members // SUB
    pitch = s_ref.shape[0] // members
    pitch_b = b_ref.shape[0] // members
    half_cols = cols_north // 2
    half = cols_east * half_cols
    deep = half_cols // SPAN + 2

    def fetch(a):
        return pltpu.make_async_copy(state_ref.at[:, a], state_v.at[:, a], in_sem.at[a])

    def flush(a):
        return pltpu.make_async_copy(out_v.at[:, a], out_ref.at[:, a], out_sem.at[a])

    for a in range(cols_east):
        fetch(a).start()

    row = lax.broadcasted_iota(jnp.int32, (half, LANES), 0).astype(F32)
    lane = lax.broadcasted_iota(jnp.int32, (half, LANES), 1).astype(F32)
    col_east = jnp.floor((row + 0.5) / half_cols)
    col_north = row - col_east * half_cols
    reg_east = jnp.floor((lane + 0.5) / deep)
    reg_north = lane - reg_east * deep
    hat_east = jnp.maximum(1.0 - jnp.abs(col_east + 0.5 - ((reg_east - 1.0) * SPAN + 0.5 * SPAN)) / SPAN, 0.0)
    hat_north = jnp.maximum(1.0 - jnp.abs(col_north + 0.5 - ((reg_north - 1.0) * SPAN + 0.5 * SPAN)) / SPAN, 0.0)
    hats = (hat_east * hat_north).astype(BF16)
    w_ref[:, 0:LANES] = hats
    w_ref[:, LANES:wide] = hats

    total = sums_a[...] + sums_b[...]
    prior = (members - 1) / (total[0:1, 0:1] / total[1:2, 0:1])

    sub = lax.broadcasted_iota(jnp.int32, (SUB, wide), 0)

    def gram(row0):
        return functools.reduce(lambda x, y: x + y, [g[row0 : row0 + SUB, :] for g in grams])

    pulls = [gram(pull_row + SUB * b) for b in range(blocks)]
    mean_w = [jnp.zeros((SUB, wide), F32) for _ in range(blocks)]
    row_sums = []
    for i in range(members):
        own = i // SUB
        acc_u = [gram(offsets[i] + SUB * b) for b in range(blocks - own)]
        at = sub == i % SUB
        acc_u[0] = acc_u[0] + jnp.where(at, prior, 0.0)
        acc_v = [jnp.zeros((SUB, wide), F32) for _ in range(own)] + [jnp.where(at, 1.0, 0.0)]
        for p in range(i):
            factor = u_ref[p * members + i : p * members + i + 1, :]
            for b in range(own, blocks):
                acc_u[b - own] = acc_u[b - own] - factor * u_ref[p * members + SUB * b : p * members + SUB * (b + 1), :]
            for b in range(p // SUB + 1):
                acc_v[b] = acc_v[b] - factor * v_ref[p * members + SUB * b : p * members + SUB * (b + 1), :]
        inv = lax.rsqrt(acc_u[0][i % SUB : i % SUB + 1, :])
        for b in range(own, blocks):
            u_ref[i * members + SUB * b : i * members + SUB * (b + 1), :] = acc_u[b - own] * inv
        solved, whole = None, None
        acc_v = [x * inv for x in acc_v]
        for b in range(own + 1):
            v_ref[i * members + SUB * b : i * members + SUB * (b + 1), :] = acc_v[b]
            part = acc_v[b] * pulls[b]
            solved = part if solved is None else solved + part
            whole = acc_v[b] if whole is None else whole + acc_v[b]
        solved = jnp.sum(solved, axis=0, keepdims=True)
        row_sums.append(jnp.sum(whole, axis=0, keepdims=True))
        for b in range(own + 1):
            mean_w[b] = mean_w[b] + solved * acc_v[b]

    scale = math.sqrt(members - 1)
    mean_sum = jnp.sum(functools.reduce(lambda x, y: x + y, mean_w), axis=0, keepdims=True)
    for k in range(members):
        own = k // SUB
        shift = (1.0 - mean_sum - scale * row_sums[k]) * (1.0 / members)
        parts = []
        for b in range(blocks):
            x = mean_w[b] + shift
            if b <= own:
                x = x + scale * v_ref[k * members + SUB * b : k * members + SUB * (b + 1), :]
            parts.append(x)
        parts.append(jnp.zeros((ROWS - members, wide), F32))
        table = jnp.concatenate(parts, axis=0)
        hi = table.astype(BF16)
        lo = (table - hi.astype(F32)).astype(BF16)
        for h in range(2):
            t_ref[h, k * ROWS : (k + 1) * ROWS, 0:LANES] = hi[:, h * LANES : (h + 1) * LANES]
            t_ref[h, k * ROWS : (k + 1) * ROWS, LANES:wide] = lo[:, h * LANES : (h + 1) * LANES]

    gap = jnp.zeros((LANES - 2 * ROWS, wide), BF16)
    for h in range(2):
        for k in range(0, members, 2):
            first = t_ref[h, k * ROWS : (k + 1) * ROWS, :]
            second = t_ref[h, (k + 1) * ROWS : (k + 2) * ROWS, :]
            right = jnp.concatenate([first, first, gap, second, second, gap], axis=0)
            both = lax.dot_general(w_ref[...], right, (((1,), (1,)), ((), ())), preferred_element_type=F32)
            s_ref[k * pitch + h * half : k * pitch + (h + 1) * half, :] = both[:, 0:LANES]
            s_ref[(k + 1) * pitch + h * half : (k + 1) * pitch + (h + 1) * half, :] = both[:, LANES:wide]

    low_lane = lax.broadcasted_iota(jnp.int32, (members, LANES), 1) >= ROWS
    gap_a = jnp.zeros((ROWS - members, levels), BF16)
    gap_b = jnp.zeros((LANES - 2 * ROWS, levels), BF16)

    def column_row(a, carry):
        fetch(a).wait()
        for j in range(members):
            b_ref[j * pitch_b : j * pitch_b + cols_north, :] = state_v[j, a].astype(F32)
        for b in range(cols_north):
            h, within = b // half_cols, b % half_cols
            left = s_ref[pl.ds(h * half + a * half_cols + within, members, stride=pitch), :]
            high = left.astype(BF16).astype(F32)
            left = jnp.where(low_lane, left - high, left).astype(BF16)
            column = b_ref[pl.ds(b, members, stride=pitch_b), :].astype(BF16)
            right = jnp.concatenate([column, gap_a, column, gap_a, gap_b], axis=0)
            o_ref[b * members : (b + 1) * members, :] = jnp.dot(left, right, preferred_element_type=F32)
        for k in range(members):
            out_v[k, a] = o_ref[pl.ds(k, cols_north, stride=members), :].astype(BF16)
        flush(a).start()
        return carry

    lax.fori_loop(0, cols_east, column_row, 0)
    for a in range(cols_east):
        flush(a).wait()


def analyse(grams, sums_a, sums_b, background):
    members, cols_east, cols_north, levels = background.shape
    columns = cols_east * cols_north
    count = len(grams)

    def body(*refs):
        analysis_kernel(members, refs[:count], *refs[count:])

    vmem = pl.BlockSpec(memory_space=pltpu.VMEM)
    hbm = pl.BlockSpec(memory_space=pl.ANY)
    pitch = columns + SUB
    return pl.pallas_call(
        body,
        out_shape=jax.ShapeDtypeStruct(background.shape, BF16),
        in_specs=[vmem] * (count + 2) + [hbm],
        out_specs=hbm,
        scratch_shapes=[
            pltpu.VMEM((members * members, 2 * LANES), F32),
            pltpu.VMEM((members * members, 2 * LANES), F32),
            pltpu.VMEM((2, members * ROWS, 2 * LANES), BF16),
            pltpu.VMEM((members * pitch, LANES), F32),
            pltpu.VMEM((columns // 2, 2 * LANES), BF16),
            pltpu.VMEM((members * (cols_north + SUB), levels), F32),
            pltpu.VMEM((cols_north * members, levels), F32),
            pltpu.VMEM(background.shape, BF16),
            pltpu.VMEM(background.shape, BF16),
            pltpu.SemaphoreType.DMA((cols_east,)),
            pltpu.SemaphoreType.DMA((cols_east,)),
        ],
        compiler_params=pltpu.CompilerParams(vmem_limit_bytes=48 << 20),
        name="analyse",
    )(*grams, sums_a, sums_b, background)


def rotate(value, axis, step):
    count = lax.axis_size(axis)
    return lax.ppermute(value, axis, [(i, (i + step) % count) for i in range(count)])


def slide(value, axis, step):
    count = lax.axis_size(axis)
    return lax.ppermute(value, axis, [(i, i + step) for i in range(count) if 0 <= i + step < count])


def swap(value, axis, bit):
    count = lax.axis_size(axis)
    return lax.ppermute(value, axis, [(i, i ^ bit) for i in range(count)])


def per_device(background, obs_perturb, innovation, obs_precision, obs_column, obs_count):
    members, cols_east, cols_north, levels = background.shape
    slots = obs_perturb.shape[3]
    count_east, count_north = lax.axis_size("gx"), lax.axis_size("gy")
    vmem = pl.BlockSpec(memory_space=pltpu.VMEM)
    bundle = pl.pallas_call(
        functools.partial(prep_kernel, cols_east, cols_north),
        out_shape=jax.ShapeDtypeStruct((ROWS, slots), F32),
        in_specs=[pl.BlockSpec(memory_space=pltpu.SMEM)] + [vmem] * 4,
        out_specs=vmem,
        name="prep",
    )(obs_count, obs_perturb[0, 0], innovation[0], obs_precision[0], obs_column[0])
    steps = sorted({s % count_east for s in (-2, -1, 1, 2)} - {0})
    own = jnp.concatenate([bundle] + [rotate(bundle, "gx", s) for s in steps], axis=0)
    below = slide(own, "gy", 1)
    above = slide(own, "gy", -1)

    def row_sum(bundles):
        each = bundles.reshape(-1, ROWS, slots)[:, members + 3 : members + 5, 0:LANES]
        return jnp.sum(each, axis=0)

    if len(steps) + 1 == count_east and count_north & (count_north - 1) == 0 and count_north >= 4:
        north = lax.axis_index("gy")
        beside = jnp.where(north % 2 == 0, row_sum(above), row_sum(below))
        total = row_sum(own) + beside
        bit = 2
        while 2 * bit < count_north:
            total = total + swap(total, "gy", bit)
            bit *= 2
        other = swap(total, "gy", bit)
    else:
        total = lax.psum(bundle[members + 3 : members + 5, 0:LANES], ("gx", "gy"))
        other = jnp.zeros_like(total)
    grams = [gram_table(x, members, cols_east, cols_north) for x in (own, below, above)]
    return analyse(grams, total, other, background)


def solution(mesh):
    return jax.shard_map(
        per_device,
        mesh=mesh,
        in_specs=(
            P(None, "gx", "gy", None),
            P("gx", "gy", None, None),
            P("gx", "gy", None),
            P("gx", "gy", None),
            P("gx", "gy", None),
            P("gx", "gy"),
        ),
        out_specs=P(None, "gx", "gy", None),
        check_vma=False,
    )
```

time: 177 us -> 43.8 us (0.25); the launches traced: 174 us -> 43.5 us
  matrix products: 49.9 us -> 0 us
  blocking collectives: 41.2 us -> 0 us
  other arithmetic: 36.2 us -> 0.87 us
  Pallas kernels: 0 us -> 21.5 us
  local copies, waits for them, and re-layouts: 19.8 us -> 0 us
  waiting for transfers between devices: 12.6 us -> 4.62 us
  starting transfers between devices: 8.84 us -> 15.8 us
  between operations: 5.19 us -> 0.75 us
    dot_general x12 -> x0, matrix products: 49.9 us -> none  [the longest x1 28.6 us: apply_tile(): jnp.einsum('jabl,abjk->kabl', spread, column_transform, precision=lax.Pre...]
    psum x1 -> x0, blocking collectives: 41.2 us -> none  [per_device(): lax.psum((jnp.sum(weight * values * values), jnp.sum(weight * jnp.sum(cen...]
    pallas_call x0 -> x5, Pallas kernels: none -> 21.5 us  [the longest x1 12.9 us: analyse(): pl.pallas_call(body, out_shape=jax.ShapeDtypeStruct(background.shape, BF1...]
    sub x42 -> x0, other arithmetic: 18.5 us -> none  [the longest x39 11.8 us: chol_lower(): remain = remain - column[:, None, :] * column[None, :, :]]
    reshape x3 -> x0, local copies, waits for them, and re-layouts: 9.27 us -> none  [the longest x1 6.18 us: apply_tile(): column_transform.reshape(cols_east, cols_north, members, members)]
    ppermute x8 -> x7, waiting for transfers between devices: 12.6 us -> 4.62 us  [the longest x3 4.61 us: rotate(): lax.ppermute(value, axis, [(i, (i + step) % count) for i in range(count)])]
    ppermute x8 -> x7, starting transfers between devices: 8.84 us -> 15.8 us  [the longest x2 6.41 us: swap(): return lax.ppermute(value, axis, [(i, i ^ bit) for i in range(count)])]
    reduce_sum x4 -> x3, other arithmetic: 5.6 us -> 0.04 us  [row_sum(): return jnp.sum(each, axis=0)]
  transfers between devices with their start and end apart: 8 -> 7, of which waited for: 3 -> 3; matrix products, arithmetic and copies ran while one was open for 11% -> 0% of each run, Pallas kernels for 0% -> 16%
where the time goes in v1:
time: 43.8 us; the launch traced here: 43.5 us
  Pallas kernels  21.5 us (49%)
  starting transfers between devices  15.8 us (36%)
  waiting for transfers between devices  4.62 us (11%)
  other arithmetic  0.87 us (2%)
  between operations  0.75 us (2%)
    pallas_call x1, Pallas kernels, analyse(): pl.pallas_call(body, out_shape=jax.ShapeDtypeStruct(background.shape, BF1...  12.9 us
    pallas_call x3, Pallas kernels, gram_table(): pl.pallas_call(functools.partial(gram_kernel, members, cols_east, cols_no...  7.15 us
    ppermute x2, starting transfers between devices, swap(): return lax.ppermute(value, axis, [(i, i ^ bit) for i in range(count)])  6.41 us
    ppermute x3, starting transfers between devices, rotate(): lax.ppermute(value, axis, [(i, (i + step) % count) for i in range(count)])  5.02 us
    ppermute x3, waiting for transfers between devices, rotate(): lax.ppermute(value, axis, [(i, (i + step) % count) for i in range(count)])  4.61 us
    ppermute x2, starting transfers between devices, slide(): lax.ppermute(value, axis, [(i, i + step) for i in range(count) if 0 <= i...  4.33 us
    pallas_call x1, Pallas kernels, per_device(): pl.pallas_call(functools.partial(prep_kernel, cols_east, cols_north), out...  1.48 us
  transfers between devices with their start and end apart: 7, of which 3 were waited for; matrix products, arithmetic and copies ran while one was open for 0% of the time, Pallas kernels for 16%

profile of v1, /device:TPU:0, one launch (start us, length us, event | category | flops | bytes accessed | tf_op | source)
XLA Modules:
  0.0 43.5 jit_solution(2435497695963217194)
XLA Ops:
  0.7 1.5 %prep.1 = f32[48,256]{1,0:T(8,128)} custom-call(s32[1,1]{1,0:T(1,128)S(6)} %copy.7.count_ref, bf16[40,256]{1,0:T(8,128)(2,1)} %bitcast.10, f32[1,256]{1,0:T(1,128)} %bitcast.11, f32[1,256]{1,0:T(1,128)} %bitcast.12, s32[1,256]{1,0:T(1,128)} %bitcast.13), custom_call_target="tpu_custom_call" | custom-call | tf_op jit(solution)/shard_map/prep/pallas_call | solution.py:308
  2.1 3.9 %collective-permute-start.2 = (f32[48,256]{1,0:T(8,128)}, f32[48,256]{1,0:T(8,128)S(1)}, u32[]{:S(2)}, u32[]{:S(2)}) collective-permute-start(f32[48,256]{1,0:T(8,128)} %prep.1), channel_id=1, source_target_pairs={{0,24},{8,0},{16,8},{24,16},{1,25},{9,1},{17,9},{25,17},{2,26},{10... | collective-permute-start | bytes 147464 | tf_op jit(solution)/shard_map/ppermute | solution.py:290
  6.1 0.5 %collective-permute-start.1 = (f32[48,256]{1,0:T(8,128)}, f32[48,256]{1,0:T(8,128)S(1)}, u32[]{:S(2)}, u32[]{:S(2)}) collective-permute-start(f32[48,256]{1,0:T(8,128)} %prep.1), channel_id=1, source_target_pairs={{0,16},{8,24},{16,0},{24,8},{1,17},{9,25},{17,1},{25,9},{2,18},{10... | collective-permute-start | bytes 147464 | tf_op jit(solution)/shard_map/ppermute | solution.py:290
  6.6 0.6 %collective-permute-start = (f32[48,256]{1,0:T(8,128)}, f32[48,256]{1,0:T(8,128)S(1)}, u32[]{:S(2)}, u32[]{:S(2)}) collective-permute-start(f32[48,256]{1,0:T(8,128)} %prep.1), channel_id=1, source_target_pairs={{0,8},{8,16},{16,24},{24,0},{1,9},{9,17},{17,25},{25,1},{2,10},{10... | collective-permute-start | bytes 147464 | tf_op jit(solution)/shard_map/ppermute | solution.py:290
  7.2 1.0 %collective-permute-done.2 = f32[48,256]{1,0:T(8,128)S(1)} collective-permute-done((f32[48,256]{1,0:T(8,128)}, f32[48,256]{1,0:T(8,128)S(1)}, u32[]{:S(2)}, u32[]{:S(2)}) %collective-permute-start.2) | collective-permute-done | bytes 49184 | tf_op jit(solution)/shard_map/ppermute | solution.py:290
  8.1 2.5 %collective-permute-done.1 = f32[48,256]{1,0:T(8,128)S(1)} collective-permute-done((f32[48,256]{1,0:T(8,128)}, f32[48,256]{1,0:T(8,128)S(1)}, u32[]{:S(2)}, u32[]{:S(2)}) %collective-permute-start.1) | collective-permute-done | bytes 49184 | tf_op jit(solution)/shard_map/ppermute | solution.py:290
  10.6 1.2 %collective-permute-done = f32[48,256]{1,0:T(8,128)S(1)} collective-permute-done((f32[48,256]{1,0:T(8,128)}, f32[48,256]{1,0:T(8,128)S(1)}, u32[]{:S(2)}, u32[]{:S(2)}) %collective-permute-start) | collective-permute-done | bytes 49184 | tf_op jit(solution)/shard_map/ppermute | solution.py:290
  11.8 0.8 %pad_maximum_fusion.obs_ref = f32[192,256]{1,0:T(8,128)S(1)} fusion(f32[48,256]{1,0:T(8,128)S(1)} %collective-permute-done.2, f32[48,256]{1,0:T(8,128)S(1)} %collective-permute-done.1, f32[48,256]{1,0:T(8,128)S(1)} %collective-permute-done, f32[48,256]{1,0:T(8,128)} %prep.1), kind=kLoop, calls=%fused_computation | loop fusion | flops 147456 | bytes 393216 | tf_op jit(solution)/shard_map/concatenate | solution.py:316
  12.6 1.3 %collective-permute-start.4 = (f32[192,256]{1,0:T(8,128)S(1)}, f32[192,256]{1,0:T(8,128)S(1)}, u32[]{:S(2)}, u32[]{:S(2)}) collective-permute-start(f32[192,256]{1,0:T(8,128)S(1)} %pad_maximum_fusion.obs_ref), channel_id=1, source_target_pairs={{1,0},{2,1},{3,2},{4,3},{5,4},{6,5},{7,6},{9,8},{10,9},{11,10},{12... | collective-permute-start | bytes 589832 | tf_op jit(solution)/shard_map/ppermute | solution.py:295
  13.9 3.0 %collective-permute-start.3 = (f32[192,256]{1,0:T(8,128)S(1)}, f32[192,256]{1,0:T(8,128)S(1)}, u32[]{:S(2)}, u32[]{:S(2)}) collective-permute-start(f32[192,256]{1,0:T(8,128)S(1)} %pad_maximum_fusion.obs_ref), channel_id=1, source_target_pairs={{0,1},{1,2},{2,3},{3,4},{4,5},{5,6},{6,7},{8,9},{9,10},{10,11},{11... | collective-permute-start | bytes 589832 | tf_op jit(solution)/shard_map/ppermute | solution.py:295
  16.9 2.4 %gram_table.3.refs_0_ = f32[1008,256]{1,0:T(8,128)S(1)} custom-call(f32[192,256]{1,0:T(8,128)S(1)} %pad_maximum_fusion.obs_ref), custom_call_target="tpu_custom_call" | custom-call | flops 1585446912 | bytes 2097152 | tf_op jit(solution)/shard_map/gram_table/pallas_call | solution.py:109
  19.3 0.0 collective-permute-done.4.obs_ref
  19.4 0.0 collective-permute-done.3.obs_ref
  19.4 3.8 %collective-permute-start.5 = (f32[2,128]{1,0:T(2,128)S(1)}, f32[2,128]{1,0:T(2,128)S(1)}, u32[]{:S(2)}, u32[]{:S(2)}) collective-permute-start(f32[2,128]{1,0:T(2,128)S(1)} %select_add_fusion), channel_id=1, source_target_pairs={{0,2},{1,3},{2,0},{3,1},{4,6},{5,7},{6,4},{7,5},{8,10},{9,11},{10,... | collective-permute-start | bytes 3080 | tf_op jit(solution)/shard_map/ppermute | solution.py:300
  23.2 2.4 %gram_table.4.refs_1_ = f32[1008,256]{1,0:T(8,128)S(1)} custom-call(f32[192,256]{1,0:T(8,128)S(1)} %collective-permute-done.3.obs_ref), custom_call_target="tpu_custom_call" | custom-call | flops 1585446912 | bytes 2097152 | tf_op jit(solution)/shard_map/gram_table/pallas_call | solution.py:109
  25.5 0.0 collective-permute-done.5
  25.6 2.7 %collective-permute-start.6 = (f32[2,128]{1,0:T(2,128)S(1)}, f32[2,128]{1,0:T(2,128)S(1)}, u32[]{:S(2)}, u32[]{:S(2)}) collective-permute-start(f32[2,128]{1,0:T(2,128)S(1)} %add.12.refs_3_), channel_id=1, source_target_pairs={{0,4},{1,5},{2,6},{3,7},{4,0},{5,1},{6,2},{7,3},{8,12},{9,13},{10,... | collective-permute-start | bytes 3080 | tf_op jit(solution)/shard_map/ppermute | solution.py:300
  28.2 2.4 %gram_table.5.refs_2_ = f32[1008,256]{1,0:T(8,128)S(1)} custom-call(f32[192,256]{1,0:T(8,128)S(1)} %collective-permute-done.4.obs_ref), custom_call_target="tpu_custom_call" | custom-call | flops 1585446912 | bytes 2097152 | tf_op jit(solution)/shard_map/gram_table/pallas_call | solution.py:109
  30.6 0.0 collective-permute-done.6.refs_4_
  30.6 12.9 %analyse.1 = bf16[40,16,32,128]{3,2,1,0:T(8,128)(2,1)} custom-call(f32[1008,256]{1,0:T(8,128)S(1)} %gram_table.3.refs_0_, f32[1008,256]{1,0:T(8,128)S(1)} %gram_table.4.refs_1_, f32[1008,256]{1,0:T(8,128)S(1)} %gram_table.5.refs_2_, f32[2,128]{1,0:T(2,128)S(1)} %add.12.refs_3_, f32[2,128]{1,0:T(2,128)S(1)} %collective-permute-done.6.refs_4_, ...), custom_call_target="tpu_custom_call" | custom-call | tf_op jit(solution)/shard_map/analyse/pallas_call | solution.py:265
  (5 shorter events, 0.1 us)
Async XLA Ops:
  2.1 6.0 %collective-permute-start.2 = (f32[48,256]{1,0:T(8,128)}, f32[48,256]{1,0:T(8,128)S(1)}, u32[]{:S(2)}, u32[]{:S(2)}) collective-permute-start(f32[48,256]{1,0:T(8,128)} %prep.1), channel_id=1, source_target_pairs={{0,24},{8,0},{16,8},{24,16},{1,25},{9,1},{17,9},{25,17},{2,26},{10... | collective-permute-start | bytes 147464 | tf_op jit(solution)/shard_map/ppermute | solution.py:290
  6.1 4.5 %collective-permute-start.1 = (f32[48,256]{1,0:T(8,128)}, f32[48,256]{1,0:T(8,128)S(1)}, u32[]{:S(2)}, u32[]{:S(2)}) collective-permute-start(f32[48,256]{1,0:T(8,128)} %prep.1), channel_id=1, source_target_pairs={{0,16},{8,24},{16,0},{24,8},{1,17},{9,25},{17,1},{25,9},{2,18},{10... | collective-permute-start | bytes 147464 | tf_op jit(solution)/shard_map/ppermute | solution.py:290
  6.6 5.2 %collective-permute-start = (f32[48,256]{1,0:T(8,128)}, f32[48,256]{1,0:T(8,128)S(1)}, u32[]{:S(2)}, u32[]{:S(2)}) collective-permute-start(f32[48,256]{1,0:T(8,128)} %prep.1), channel_id=1, source_target_pairs={{0,8},{8,16},{16,24},{24,0},{1,9},{9,17},{17,25},{25,1},{2,10},{10... | collective-permute-start | bytes 147464 | tf_op jit(solution)/shard_map/ppermute | solution.py:290
  12.6 6.8 %collective-permute-start.4 = (f32[192,256]{1,0:T(8,128)S(1)}, f32[192,256]{1,0:T(8,128)S(1)}, u32[]{:S(2)}, u32[]{:S(2)}) collective-permute-start(f32[192,256]{1,0:T(8,128)S(1)} %pad_maximum_fusion.obs_ref), channel_id=1, source_target_pairs={{1,0},{2,1},{3,2},{4,3},{5,4},{6,5},{7,6},{9,8},{10,9},{11,10},{12... | collective-permute-start | bytes 589832 | tf_op jit(solution)/shard_map/ppermute | solution.py:295
  13.9 5.5 %collective-permute-start.3 = (f32[192,256]{1,0:T(8,128)S(1)}, f32[192,256]{1,0:T(8,128)S(1)}, u32[]{:S(2)}, u32[]{:S(2)}) collective-permute-start(f32[192,256]{1,0:T(8,128)S(1)} %pad_maximum_fusion.obs_ref), channel_id=1, source_target_pairs={{0,1},{1,2},{2,3},{3,4},{4,5},{5,6},{6,7},{8,9},{9,10},{10,11},{11... | collective-permute-start | bytes 589832 | tf_op jit(solution)/shard_map/ppermute | solution.py:295
  19.4 6.2 %collective-permute-start.5 = (f32[2,128]{1,0:T(2,128)S(1)}, f32[2,128]{1,0:T(2,128)S(1)}, u32[]{:S(2)}, u32[]{:S(2)}) collective-permute-start(f32[2,128]{1,0:T(2,128)S(1)} %select_add_fusion), channel_id=1, source_target_pairs={{0,2},{1,3},{2,0},{3,1},{4,6},{5,7},{6,4},{7,5},{8,10},{9,11},{10,... | collective-permute-start | bytes 3080 | tf_op jit(solution)/shard_map/ppermute | solution.py:300
  25.6 5.1 %collective-permute-start.6 = (f32[2,128]{1,0:T(2,128)S(1)}, f32[2,128]{1,0:T(2,128)S(1)}, u32[]{:S(2)}, u32[]{:S(2)}) collective-permute-start(f32[2,128]{1,0:T(2,128)S(1)} %add.12.refs_3_), channel_id=1, source_target_pairs={{0,4},{1,5},{2,6},{3,7},{4,0},{5,1},{6,2},{7,3},{8,12},{9,13},{10,... | collective-permute-start | bytes 3080 | tf_op jit(solution)/shard_map/ppermute | solution.py:300

commit v2 on v1

v2 whole, which is shorter than its diff:
```python
import functools
import math

import jax
import jax.numpy as jnp
from jax import lax
from jax.experimental import pallas as pl
from jax.experimental.pallas import tpu as pltpu
from jax.sharding import PartitionSpec as P

SPAN = 2
LANES = 128
SUB = 8
ROWS = 48
SLOT = 64
F32 = jnp.float32
BF16 = jnp.bfloat16


def pair_rows(members):
    offsets, total = [], 0
    for i in range(members):
        offsets.append(total)
        total += members - (i // SUB) * SUB
    pull = total
    total += members
    return offsets, pull, -(-total // 16) * 16


def prep_kernel(
    cols_east, cols_north, count_ref, perturb_hbm, innov_hbm, prec_hbm, column_hbm, out_ref,
    perturb_ref, innov_ref, prec_ref, column_ref, sem,
):
    pairs = ((perturb_hbm, perturb_ref), (innov_hbm, innov_ref), (prec_hbm, prec_ref), (column_hbm, column_ref))
    copies = [pltpu.make_async_copy(src, dst, sem.at[n]) for n, (src, dst) in enumerate(pairs)]
    for copy in copies:
        copy.start()
    for copy in copies:
        copy.wait()
    members, slots = perturb_ref.shape
    tile_east, tile_north = lax.axis_index("gx"), lax.axis_index("gy")
    values, column = innov_ref[...], column_ref[...].astype(F32)
    spread = perturb_ref[...].astype(F32)
    spread = spread - jnp.sum(spread, axis=0, keepdims=True) / members
    lane = lax.broadcasted_iota(jnp.int32, (1, slots), 1)
    weight = jnp.where(lane < count_ref[0, 0], prec_ref[...], 0.0)
    root = jnp.sqrt(weight)
    east = jnp.floor((column + 0.5) * (1.0 / cols_north))
    north = column - east * cols_north + (tile_north * cols_north).astype(F32) + 0.5
    east = east + (tile_east * cols_east).astype(F32) + 0.5
    numer = jnp.sum(weight * values * values, axis=1, keepdims=True)
    variance = jnp.sum(spread * spread, axis=0, keepdims=True)
    denom = jnp.sum(weight * variance, axis=1, keepdims=True) / (members - 1)
    out_ref[0:members, :] = spread * root
    row = lax.broadcasted_iota(jnp.int32, (ROWS - members, slots), 0)
    rest = jnp.zeros((ROWS - members, slots), F32)
    for place, value in enumerate((values * root, east, north, numer, denom)):
        rest = jnp.where(row == place, value, rest)
    out_ref[members:ROWS, :] = rest


def gram_kernel(members, cols_east, cols_north, obs_ref, out_ref, lhs_hi, lhs_lo, rhs_hi, rhs_lo):
    tiles = obs_ref.shape[0] // ROWS
    slots = obs_ref.shape[1]
    offsets, pull_row, total = pair_rows(members)
    regions_north = cols_north // SPAN
    deep = regions_north // 2 + 2
    lanes = 2 * LANES
    tile_east, tile_north = lax.axis_index("gx"), lax.axis_index("gy")
    count_north = lax.axis_size("gy")
    lane = lax.broadcasted_iota(jnp.int32, (1, lanes), 1)
    half = (lane >= LANES).astype(jnp.int32)
    inner = (lane - half * LANES).astype(F32)
    place_east = jnp.floor((inner + 0.5) / deep)
    place_north = inner - place_east * deep
    centre_east = (tile_east * cols_east).astype(F32) + (place_east - 1.0) * SPAN + 0.5 * SPAN
    place_north = place_north + (tile_north * regions_north + half * (regions_north // 2) - 1).astype(F32)
    place_north = jnp.clip(place_north, 0.0, float(count_north * regions_north - 1))
    centre_north = place_north * SPAN + 0.5 * SPAN
    period = float(lax.axis_size("gx") * cols_east)
    radius = float(cols_east)
    inv_radius = 1.0 / radius
    centre_north = centre_north * inv_radius

    def build(t):
        base = t * ROWS
        place = jnp.transpose(obs_ref[base + members : base + ROWS, :])
        east, north = place[:, 1:2], place[:, 2:3] * inv_radius
        away = jnp.abs(east - centre_east)
        away = jnp.minimum(away, period - away) * inv_radius
        up = north - centre_north
        near = jnp.maximum(1.0 - away * away - up * up, 0.0)
        taper = near * near
        span = slice(t * slots, (t + 1) * slots)
        hi = taper.astype(BF16)
        rhs_hi[span, :] = hi
        rhs_lo[span, :] = (taper - hi.astype(F32)).astype(BF16)
        for i in range(0, members, 2):
            first = (i // SUB) * SUB
            rows = obs_ref[base + first : base + members, :]
            table = jnp.concatenate(
                [obs_ref[base + i : base + i + 1, :] * rows, obs_ref[base + i + 1 : base + i + 2, :] * rows], axis=0
            )
            hi = table.astype(BF16)
            lhs_hi[offsets[i] : offsets[i] + table.shape[0], span] = hi
            lhs_lo[offsets[i] : offsets[i] + table.shape[0], span] = (table - hi.astype(F32)).astype(BF16)
        table = obs_ref[base + members : base + members + 1, :] * obs_ref[base : base + members, :]
        table = jnp.concatenate([table, jnp.zeros((total - pull_row - members, slots), F32)], axis=0)
        hi = table.astype(BF16)
        lhs_hi[pull_row:total, span] = hi
        lhs_lo[pull_row:total, span] = (table - hi.astype(F32)).astype(BF16)

    def multiply(t):
        span = slice(t * slots, (t + 1) * slots)
        left = jnp.concatenate([lhs_hi[:, span], lhs_lo[:, span], lhs_hi[:, span]], axis=1)
        right = jnp.concatenate([rhs_hi[span, :], rhs_hi[span, :], rhs_lo[span, :]], axis=0)
        return jnp.dot(left, right, preferred_element_type=F32)

    build(0)
    for t in range(tiles):
        if t + 1 < tiles:
            build(t + 1)
        if t == 0:
            out_ref[...] = multiply(t)
        else:
            out_ref[...] += multiply(t)


def gram_table(bundles, members, cols_east, cols_north):
    total = pair_rows(members)[2]
    deep = bundles.shape[0] // ROWS * bundles.shape[1]
    return pl.pallas_call(
        functools.partial(gram_kernel, members, cols_east, cols_north),
        out_shape=jax.ShapeDtypeStruct((total, 2 * LANES), F32),
        in_specs=[pl.BlockSpec(memory_space=pltpu.VMEM)],
        out_specs=pl.BlockSpec(memory_space=pltpu.VMEM),
        scratch_shapes=[
            pltpu.VMEM((total, deep), BF16),
            pltpu.VMEM((total, deep), BF16),
            pltpu.VMEM((deep, 2 * LANES), BF16),
            pltpu.VMEM((deep, 2 * LANES), BF16),
        ],
        compiler_params=pltpu.CompilerParams(vmem_limit_bytes=16 << 20),
        cost_estimate=pl.CostEstimate(flops=6 * total * deep * 2 * LANES, bytes_accessed=1 << 21, transcendentals=0),
        name="gram_table",
    )(bundles)


def columns_kernel(state_ref, out_ref, state_v, even_ref, odd_ref, in_sem):
    members, cols_east, cols_north, levels = state_v.shape
    pitch = even_ref.shape[0] // members

    def fetch(a):
        return pltpu.make_async_copy(state_ref.at[:, a], state_v.at[:, a], in_sem.at[a])

    for a in range(cols_east):
        fetch(a).start()
    gap = jnp.zeros((ROWS - members, levels), BF16)

    def load(a, ref):
        fetch(a).wait()
        for j in range(members):
            ref[j * pitch : j * pitch + cols_north, :] = state_v[j, a].astype(F32)

    def store(a, ref):
        for b in range(cols_north):
            column = ref[pl.ds(b, members, stride=pitch), :].astype(BF16)
            out_ref[a, b] = jnp.concatenate([column, gap], axis=0)

    def pair(t, carry):
        load(2 * t, even_ref)
        load(2 * t + 1, odd_ref)
        store(2 * t, even_ref)
        store(2 * t + 1, odd_ref)
        return carry

    lax.fori_loop(0, cols_east // 2, pair, 0)


def by_column(background):
    members, cols_east, cols_north, levels = background.shape
    shape = (cols_east, cols_north, ROWS, levels)
    return pl.pallas_call(
        columns_kernel,
        out_shape=jax.ShapeDtypeStruct(shape, BF16),
        in_specs=[pl.BlockSpec(memory_space=pltpu.HBM)],
        out_specs=pl.BlockSpec(memory_space=pltpu.VMEM),
        scratch_shapes=[
            pltpu.VMEM(background.shape, BF16),
            pltpu.VMEM((members * (cols_north + 1), levels), F32),
            pltpu.VMEM((members * (cols_north + 1), levels), F32),
            pltpu.SemaphoreType.DMA((cols_east,)),
        ],
        compiler_params=pltpu.CompilerParams(vmem_limit_bytes=20 << 20),
        cost_estimate=pl.CostEstimate(flops=0, bytes_accessed=12 << 20, transcendentals=0),
        name="columns",
    )(pltpu.with_memory_space_constraint(background, pltpu.HBM))


def analysis_kernel(
    members, grams, sums_a, sums_b, column_ref, out_ref, u_ref, v_ref, t_ref, s_ref, m_ref, w_ref, mean_ref, o_refs, out_v, out_sem
):
    _, cols_east, cols_north, levels = out_v.shape
    offsets, pull_row, _ = pair_rows(members)
    wide = 2 * LANES
    blocks = members // SUB
    pitch = cols_east * cols_north + 1
    half_cols = cols_north // 2
    half = cols_east * half_cols
    deep = half_cols // SPAN + 2

    def flush(a):
        return pltpu.make_async_copy(out_v.at[:, a], out_ref.at[:, a], out_sem.at[a])

    row = lax.broadcasted_iota(jnp.int32, (half, LANES), 0).astype(F32)
    lane = lax.broadcasted_iota(jnp.int32, (half, LANES), 1).astype(F32)
    col_east = jnp.floor((row + 0.5) / half_cols)
    col_north = row - col_east * half_cols
    reg_east = jnp.floor((lane + 0.5) / deep)
    reg_north = lane - reg_east * deep
    hat_east = jnp.maximum(1.0 - jnp.abs(col_east + 0.5 - ((reg_east - 1.0) * SPAN + 0.5 * SPAN)) / SPAN, 0.0)
    hat_north = jnp.maximum(1.0 - jnp.abs(col_north + 0.5 - ((reg_north - 1.0) * SPAN + 0.5 * SPAN)) / SPAN, 0.0)
    hats = (hat_east * hat_north).astype(BF16)
    w_ref[:, 0:LANES] = hats
    w_ref[:, LANES:wide] = hats

    total = sums_a[...] + sums_b[...]
    prior = (members - 1) / (total[0:1, 0:1] / total[1:2, 0:1])
    sub = lax.broadcasted_iota(jnp.int32, (SUB, wide), 0)
    gap = jnp.zeros((SLOT - ROWS, wide), BF16)
    fold = -(-members // (2 * SUB)) * SUB

    def gram(row0):
        return functools.reduce(lambda x, y: x + y, [g[row0 : row0 + SUB, :] for g in grams])

    def part(h, k):
        return t_ref[h, k * ROWS : (k + 1) * ROWS, :]

    def put(k, blocks_k):
        table = jnp.concatenate(blocks_k + [jnp.zeros((ROWS - members, wide), F32)], axis=0)
        hi = table.astype(BF16)
        lo = (table - hi.astype(F32)).astype(BF16)
        for h in range(2):
            t_ref[h, k * ROWS : (k + 1) * ROWS, 0:LANES] = hi[:, h * LANES : (h + 1) * LANES]
            t_ref[h, k * ROWS : (k + 1) * ROWS, LANES:wide] = lo[:, h * LANES : (h + 1) * LANES]

    def spread(h, right):
        return lax.dot_general(w_ref[...], right, (((1,), (1,)), ((), ())), preferred_element_type=F32)

    scale = math.sqrt(members - 1)
    mean_ref[...] = jnp.zeros_like(mean_ref)

    def factor_rows(start, stop):
        for i in range(start, stop):
            own = i // SUB
            acc_u = [gram(offsets[i] + SUB * b) for b in range(blocks - own)]
            at = sub == i % SUB
            acc_u[0] = acc_u[0] + jnp.where(at, prior, 0.0)
            acc_v = [jnp.zeros((SUB, wide), F32) for _ in range(own)] + [jnp.where(at, 1.0, 0.0)]
            for p in range(i):
                row = p * members
                factor = u_ref[row + i : row + i + 1, :]
                for b in range(own, blocks):
                    acc_u[b - own] = acc_u[b - own] - factor * u_ref[row + SUB * b : row + SUB * (b + 1), :]
                for b in range(p // SUB + 1):
                    acc_v[b] = acc_v[b] - factor * v_ref[row + SUB * b : row + SUB * (b + 1), :]
            inv = lax.rsqrt(acc_u[0][i % SUB : i % SUB + 1, :])
            for b in range(own, blocks):
                u_ref[i * members + SUB * b : i * members + SUB * (b + 1), :] = acc_u[b - own] * inv
            for b in range(own + 1):
                v_ref[i * members + SUB * b : i * members + SUB * (b + 1), :] = acc_v[b] * inv

    def put_rows(start, stop):
        most = (stop - 1) // SUB + 1
        pulls = [gram(pull_row + SUB * b) for b in range(most)]
        mean_w = [mean_ref[SUB * b : SUB * (b + 1), :] for b in range(most)]
        for i in range(start, stop):
            count = i // SUB + 1
            rows = [v_ref[i * members + SUB * b : i * members + SUB * (b + 1), :] for b in range(count)]
            solved = functools.reduce(lambda x, y: x + y, [x * y for x, y in zip(rows, pulls)])
            solved = jnp.sum(solved, axis=0, keepdims=True)
            shift = jnp.sum(functools.reduce(lambda x, y: x + y, rows), axis=0, keepdims=True) * (-scale / members)
            for b in range(count):
                mean_w[b] = mean_w[b] + solved * rows[b]
            rows = [x * scale + shift for x in rows]
            put(i, rows + [jnp.broadcast_to(shift, (SUB, wide))] * (blocks - count))
        for b in range(most):
            mean_ref[SUB * b : SUB * (b + 1), :] = mean_w[b]

    def spread_rows(k):
        for h in range(2):
            sides = []
            for n in (k, k + 1):
                other = part(h, n + fold) if n + fold < members else jnp.zeros((ROWS, wide), BF16)
                sides += [part(h, n), gap, other, gap]
            both = spread(h, jnp.concatenate(sides, axis=0))
            s_ref[k * pitch + h * half : k * pitch + (h + 1) * half, :] = both[:, 0:LANES]
            s_ref[(k + 1) * pitch + h * half : (k + 1) * pitch + (h + 1) * half, :] = both[:, LANES:wide]

    def spread_mean():
        mean_w = [mean_ref[SUB * b : SUB * (b + 1), :] for b in range(blocks)]
        mean_sum = jnp.sum(functools.reduce(lambda x, y: x + y, mean_w), axis=0, keepdims=True)
        shift = (1.0 - mean_sum) * (1.0 / members)
        put(members, [x + shift for x in mean_w])
        for h in range(2):
            right = jnp.concatenate([part(h, members), gap, part(h, members), gap], axis=0)
            m_ref[h * half : (h + 1) * half, :] = spread(h, right)

    for i in range(members):
        factor_rows(i, i + 1)
        put_rows(i, i + 1)
        if i % 2 and i >= fold:
            spread_rows(i - fold - 1)
    for k in range(members - fold, fold, 2):
        spread_rows(k)
    spread_mean()
    lower_lane = lax.broadcasted_iota(jnp.int32, (fold, LANES), 1) < SLOT
    blank = jnp.zeros((SLOT - ROWS, 2 * levels), BF16)
    pitch_o = members + 1

    def matrix(a, b):
        h, within = b // half_cols, b % half_cols
        place = h * half + a * half_cols + within
        value = s_ref[pl.ds(place, fold, stride=pitch), :] + m_ref[pl.ds(place, 1), :]
        high = value.astype(BF16).astype(F32)
        low = value - high
        turned = pltpu.roll(jnp.where(lower_lane, low, high), SLOT, 1)
        first = jnp.where(lower_lane, high, turned)
        second = jnp.where(lower_lane, turned, low)
        return [first, second[0 : members - fold, :]]

    def apply(a, b, o_ref):
        left = jnp.concatenate(matrix(a, b) + matrix(a, b + 1), axis=0).astype(BF16)
        right = jnp.concatenate([column_ref[a, b], column_ref[a, b + 1]], axis=1)
        right = jnp.concatenate([right, blank, right, blank], axis=0)
        both = jnp.dot(left, right, preferred_element_type=F32)
        o_ref[b * pitch_o : b * pitch_o + members, :] = both[:members, 0:levels]
        o_ref[(b + 1) * pitch_o : (b + 1) * pitch_o + members, :] = both[members:, levels:]

    def emit(a, k, o_ref):
        out_v[k, a] = o_ref[pl.ds(k, cols_north, stride=pitch_o), :].astype(BF16)

    def step(a, to_ref, from_ref):
        done = 0
        for b in range(0, cols_north, 2):
            if to_ref is not None:
                apply(a, b, to_ref)
            if from_ref is not None:
                upto = members * (b + 2) // cols_north
                for k in range(done, upto):
                    emit(a - 1, k, from_ref)
                done = upto
        if from_ref is not None:
            flush(a - 1).start()

    even, odd = o_refs
    step(0, even, None)

    def column_rows(t, carry):
        step(2 * t + 1, odd, even)
        step(2 * t + 2, even, odd)
        return carry

    lax.fori_loop(0, cols_east // 2 - 1, column_rows, 0)
    step(cols_east - 1, odd, even)
    step(cols_east, None, odd)
    for a in range(cols_east):
        flush(a).wait()


def analyse(grams, sums_a, sums_b, columns, members):
    cols_east, cols_north, _, levels = columns.shape
    count = cols_east * cols_north
    tables = len(grams)

    def body(*refs):
        rest = refs[tables:]
        analysis_kernel(members, refs[:tables], *rest[:11], rest[11:13], *rest[13:])

    vmem = pl.BlockSpec(memory_space=pltpu.VMEM)
    hbm = pl.BlockSpec(memory_space=pltpu.HBM)
    pitch = count + 1
    shape = (members, cols_east, cols_north, levels)
    return pl.pallas_call(
        body,
        out_shape=jax.ShapeDtypeStruct(shape, BF16),
        in_specs=[vmem] * (tables + 3),
        out_specs=hbm,
        scratch_shapes=[
            pltpu.VMEM((members * members, 2 * LANES), F32),
            pltpu.VMEM((members * members, 2 * LANES), F32),
            pltpu.VMEM((2, (members + 1) * ROWS, 2 * LANES), BF16),
            pltpu.VMEM((-(-members // (2 * SUB)) * SUB * pitch, LANES), F32),
            pltpu.VMEM((count, LANES), F32),
            pltpu.VMEM((count // 2, 2 * LANES), BF16),
            pltpu.VMEM((members, 2 * LANES), F32),
            pltpu.VMEM((cols_north * (members + 1), levels), F32),
            pltpu.VMEM((cols_north * (members + 1), levels), F32),
            pltpu.VMEM(shape, BF16),
            pltpu.SemaphoreType.DMA((cols_east,)),
        ],
        compiler_params=pltpu.CompilerParams(vmem_limit_bytes=30 << 20),
        name="analyse",
    )(*grams, sums_a, sums_b, columns)


def rotate(value, axis, step):
    count = lax.axis_size(axis)
    return lax.ppermute(value, axis, [(i, (i + step) % count) for i in range(count)])


def slide(value, axis, step):
    count = lax.axis_size(axis)
    return lax.ppermute(value, axis, [(i, i + step) for i in range(count) if 0 <= i + step < count])


def swap(value, axis, bit):
    count = lax.axis_size(axis)
    return lax.ppermute(value, axis, [(i, i ^ bit) for i in range(count)])


def per_device(background, obs_perturb, innovation, obs_precision, obs_column, obs_count):
    members, cols_east, cols_north, levels = background.shape
    slots = obs_perturb.shape[3]
    count_east, count_north = lax.axis_size("gx"), lax.axis_size("gy")
    vmem = pl.BlockSpec(memory_space=pltpu.VMEM)
    hbm = pl.BlockSpec(memory_space=pltpu.HBM)
    inputs = (obs_perturb[0, 0], innovation[0], obs_precision[0], obs_column[0])
    bundle = pl.pallas_call(
        functools.partial(prep_kernel, cols_east, cols_north),
        out_shape=jax.ShapeDtypeStruct((ROWS, slots), F32),
        in_specs=[pl.BlockSpec(memory_space=pltpu.SMEM)] + [hbm] * 4,
        out_specs=vmem,
        scratch_shapes=[pltpu.VMEM(x.shape, x.dtype) for x in inputs] + [pltpu.SemaphoreType.DMA((4,))],
        compiler_params=pltpu.CompilerParams(vmem_limit_bytes=2 << 20),
        name="prep",
    )(obs_count, *(pltpu.with_memory_space_constraint(x, pltpu.HBM) for x in inputs))
    steps = sorted({s % count_east for s in (-2, -1, 1, 2)} - {0})
    around = [rotate(bundle, "gx", s) for s in steps]
    columns = by_column(background)
    own = jnp.concatenate([bundle] + around, axis=0)
    below = slide(own, "gy", 1)
    above = slide(own, "gy", -1)

    def row_sum(bundles):
        each = bundles.reshape(-1, ROWS, slots)[:, members + 3 : members + 5, 0:LANES]
        return jnp.sum(each, axis=0)

    if len(steps) + 1 == count_east and count_north == 8:
        mine = row_sum(own)
        far = swap(mine, "gy", 2), swap(mine, "gy", 4)
        beside = jnp.where(lax.axis_index("gy") % 2 == 0, row_sum(above), row_sum(below))
        total = (mine + beside) + (far[0] + far[1])
        other = swap(total, "gy", 7)
    else:
        total = lax.psum(bundle[members + 3 : members + 5, 0:LANES], ("gx", "gy"))
        other = jnp.zeros_like(total)
    grams = [gram_table(x, members, cols_east, cols_north) for x in (own, below, above)]
    return analyse(grams, total, other, columns, members)


def solution(mesh):
    return jax.shard_map(
        per_device,
        mesh=mesh,
        in_specs=(
            P(None, "gx", "gy", None),
            P("gx", "gy", None, None),
            P("gx", "gy", None),
            P("gx", "gy", None),
            P("gx", "gy", None),
            P("gx", "gy"),
        ),
        out_specs=P(None, "gx", "gy", None),
        check_vma=False,
    )
```

time: 43.8 us -> 37.9 us (0.87)
  the two profiles are of different devices: /device:TPU:0 before, /device:TPU:1 now
where the time goes in v2:
time: 37.9 us; the launch traced here: 37.7 us
  Pallas kernels  19.7 us (52%)
  starting transfers between devices  16.1 us (42%)
  waiting for transfers between devices  1.05 us (3%)
  between operations  0.76 us (2%)
    pallas_call x1, Pallas kernels, analyse(): pl.pallas_call(body, out_shape=jax.ShapeDtypeStruct(shape, BF16), in_spec...  9.25 us
    pallas_call x3, Pallas kernels, gram_table(): pl.pallas_call(functools.partial(gram_kernel, members, cols_east, cols_no...  6.84 us
    ppermute x2, starting transfers between devices, slide(): lax.ppermute(value, axis, [(i, i + step) for i in range(count) if 0 <= i...  6.79 us
    ppermute x3, starting transfers between devices, swap(): return lax.ppermute(value, axis, [(i, i ^ bit) for i in range(count)])  5.75 us
    ppermute x3, starting transfers between devices, rotate(): lax.ppermute(value, axis, [(i, (i + step) % count) for i in range(count)])  3.58 us
    pallas_call x1, Pallas kernels, by_column(): pl.pallas_call(columns_kernel, out_shape=jax.ShapeDtypeStruct(shape, BF16...  2.76 us
    pallas_call x1, Pallas kernels, per_device(): pl.pallas_call(functools.partial(prep_kernel, cols_east, cols_north), out...  0.88 us
    ppermute x3, waiting for transfers between devices, rotate(): lax.ppermute(value, axis, [(i, (i + step) % count) for i in range(count)])  0.76 us
  transfers between devices with their start and end apart: 8, of which 2 were waited for; matrix products, arithmetic and copies ran while one was open for 0% of the time, Pallas kernels for 25%

profile of v2, /device:TPU:1, one launch (start us, length us, event | category | flops | bytes accessed | tf_op | source)
XLA Modules:
  0.0 37.7 jit_solution(11360810512259140034)
XLA Ops:
  0.7 0.9 %prep.1 = f32[48,256]{1,0:T(8,128)S(1)} custom-call(s32[1,1]{1,0:T(1,128)S(6)} %copy.7.count_ref, bf16[40,256]{1,0:T(8,128)(2,1)} %bitcast.10, f32[1,256]{1,0:T(1,128)} %bitcast.11, f32[1,256]{1,0:T(1,128)} %bitcast.12, s32[1,256]{1,0:T(1,128)} %bitcast.13), custom_call_target="tpu_custom_call" | custom-call | tf_op jit(solution)/shard_map/prep/pallas_call | solution.py:429
  1.5 3.0 %collective-permute-start.2 = (f32[48,256]{1,0:T(8,128)S(1)}, f32[48,256]{1,0:T(8,128)S(1)}, u32[]{:S(2)}, u32[]{:S(2)}) collective-permute-start(f32[48,256]{1,0:T(8,128)S(1)} %prep.1), channel_id=1, source_target_pairs={{0,24},{8,0},{16,8},{24,16},{1,25},{9,1},{17,9},{25,17},{2,26},{10... | collective-permute-start | bytes 147464 | tf_op jit(solution)/shard_map/ppermute | solution.py:409
  4.6 0.2 collective-permute-start.1
  4.8 0.3 collective-permute-start
  5.1 2.8 %columns.1.refs_5_ = bf16[16,32,48,128]{3,2,1,0:T(8,128)(2,1)S(1)} custom-call(bf16[40,16,32,128]{3,2,1,0:T(8,128)(2,1)} %state_ref.1), custom_call_target="tpu_custom_call" | custom-call | bytes 12582912 | tf_op jit(solution)/shard_map/columns/pallas_call | solution.py:183
  7.9 0.0 collective-permute-done.2
  7.9 0.0 collective-permute-done.1
  7.9 0.8 %collective-permute-done = f32[48,256]{1,0:T(8,128)S(1)} collective-permute-done((f32[48,256]{1,0:T(8,128)S(1)}, f32[48,256]{1,0:T(8,128)S(1)}, u32[]{:S(2)}, u32[]{:S(2)}) %collective-permute-start) | collective-permute-done | bytes 49184 | tf_op jit(solution)/shard_map/ppermute | solution.py:409
  8.7 4.3 %collective-permute-start.4 = (f32[192,256]{1,0:T(8,128)S(1)}, f32[192,256]{1,0:T(8,128)S(1)}, u32[]{:S(2)}, u32[]{:S(2)}) collective-permute-start(f32[192,256]{1,0:T(8,128)S(1)} %pad_maximum_fusion.obs_ref), channel_id=1, source_target_pairs={{1,0},{2,1},{3,2},{4,3},{5,4},{6,5},{7,6},{9,8},{10,9},{11,10},{12... | collective-permute-start | bytes 589832 | tf_op jit(solution)/shard_map/ppermute | solution.py:414
  13.0 2.4 %collective-permute-start.6 = (f32[2,128]{1,0:T(2,128)S(1)}, f32[2,128]{1,0:T(2,128)S(1)}, u32[]{:S(2)}, u32[]{:S(2)}) collective-permute-start(f32[2,128]{1,0:T(2,128)S(1)} %slice_reduce_fusion.2), channel_id=1, source_target_pairs={{0,4},{1,5},{2,6},{3,7},{4,0},{5,1},{6,2},{7,3},{8,12},{9,13},{10,... | collective-permute-start | bytes 3080 | tf_op jit(solution)/shard_map/ppermute | solution.py:419
  15.3 1.3 %collective-permute-start.5 = (f32[2,128]{1,0:T(2,128)S(1)}, f32[2,128]{1,0:T(2,128)S(1)}, u32[]{:S(2)}, u32[]{:S(2)}) collective-permute-start(f32[2,128]{1,0:T(2,128)S(1)} %slice_reduce_fusion.2), channel_id=1, source_target_pairs={{0,2},{1,3},{2,0},{3,1},{4,6},{5,7},{6,4},{7,5},{8,10},{9,11},{10,... | collective-permute-start | bytes 3080 | tf_op jit(solution)/shard_map/ppermute | solution.py:419
  16.7 2.5 %collective-permute-start.3 = (f32[192,256]{1,0:T(8,128)S(1)}, f32[192,256]{1,0:T(8,128)S(1)}, u32[]{:S(2)}, u32[]{:S(2)}) collective-permute-start(f32[192,256]{1,0:T(8,128)S(1)} %pad_maximum_fusion.obs_ref), channel_id=1, source_target_pairs={{0,1},{1,2},{2,3},{3,4},{4,5},{5,6},{6,7},{8,9},{9,10},{10,11},{11... | collective-permute-start | bytes 589832 | tf_op jit(solution)/shard_map/ppermute | solution.py:414
  19.2 2.3 %gram_table.3.refs_0_ = f32[1008,256]{1,0:T(8,128)S(1)} custom-call(f32[192,256]{1,0:T(8,128)S(1)} %pad_maximum_fusion.obs_ref), custom_call_target="tpu_custom_call" | custom-call | flops 1585446912 | bytes 2097152 | tf_op jit(solution)/shard_map/gram_table/pallas_call | solution.py:132
  21.5 0.0 collective-permute-done.4.obs_ref
  21.5 0.3 collective-permute-done.3.obs_ref
  21.8 0.0 collective-permute-done.6
  21.8 0.0 collective-permute-done.5
  21.8 2.1 %collective-permute-start.7 = (f32[2,128]{1,0:T(2,128)S(1)}, f32[2,128]{1,0:T(2,128)S(1)}, u32[]{:S(2)}, u32[]{:S(2)}) collective-permute-start(f32[2,128]{1,0:T(2,128)S(1)} %add_add_fusion.refs_3_), channel_id=1, source_target_pairs={{0,7},{1,6},{2,5},{3,4},{4,3},{5,2},{6,1},{7,0},{8,15},{9,14},{10,... | collective-permute-start | bytes 3080 | tf_op jit(solution)/shard_map/ppermute | solution.py:419
  23.9 2.3 %gram_table.4.refs_1_ = f32[1008,256]{1,0:T(8,128)S(1)} custom-call(f32[192,256]{1,0:T(8,128)S(1)} %collective-permute-done.3.obs_ref), custom_call_target="tpu_custom_call" | custom-call | flops 1585446912 | bytes 2097152 | tf_op jit(solution)/shard_map/gram_table/pallas_call | solution.py:132
  26.2 2.3 %gram_table.5.refs_2_ = f32[1008,256]{1,0:T(8,128)S(1)} custom-call(f32[192,256]{1,0:T(8,128)S(1)} %collective-permute-done.4.obs_ref), custom_call_target="tpu_custom_call" | custom-call | flops 1585446912 | bytes 2097152 | tf_op jit(solution)/shard_map/gram_table/pallas_call | solution.py:132
  28.4 0.0 collective-permute-done.7.refs_4_
  28.5 9.2 %analyse.1 = bf16[40,16,32,128]{3,2,1,0:T(8,128)(2,1)} custom-call(f32[1008,256]{1,0:T(8,128)S(1)} %gram_table.3.refs_0_, f32[1008,256]{1,0:T(8,128)S(1)} %gram_table.4.refs_1_, f32[1008,256]{1,0:T(8,128)S(1)} %gram_table.5.refs_2_, f32[2,128]{1,0:T(2,128)S(1)} %add_add_fusion.refs_3_, f32[2,128]{1,0:T(2,128)S(1)} %collective-permute-done.7.refs_4_, ...), custom_call_target="tpu_custom_call" | custom-call | tf_op jit(solution)/shard_map/analyse/pallas_call | solution.py:384
  (5 shorter events, 0.1 us)
Async XLA Ops:
  1.5 6.4 %collective-permute-start.2 = (f32[48,256]{1,0:T(8,128)S(1)}, f32[48,256]{1,0:T(8,128)S(1)}, u32[]{:S(2)}, u32[]{:S(2)}) collective-permute-start(f32[48,256]{1,0:T(8,128)S(1)} %prep.1), channel_id=1, source_target_pairs={{0,24},{8,0},{16,8},{24,16},{1,25},{9,1},{17,9},{25,17},{2,26},{10... | collective-permute-start | bytes 147464 | tf_op jit(solution)/shard_map/ppermute | solution.py:409
  4.6 3.3 %collective-permute-start.1 = (f32[48,256]{1,0:T(8,128)S(1)}, f32[48,256]{1,0:T(8,128)S(1)}, u32[]{:S(2)}, u32[]{:S(2)}) collective-permute-start(f32[48,256]{1,0:T(8,128)S(1)} %prep.1), channel_id=1, source_target_pairs={{0,16},{8,24},{16,0},{24,8},{1,17},{9,25},{17,1},{25,9},{2,18},{10... | collective-permute-start | bytes 147464 | tf_op jit(solution)/shard_map/ppermute | solution.py:409
  4.8 3.9 %collective-permute-start = (f32[48,256]{1,0:T(8,128)S(1)}, f32[48,256]{1,0:T(8,128)S(1)}, u32[]{:S(2)}, u32[]{:S(2)}) collective-permute-start(f32[48,256]{1,0:T(8,128)S(1)} %prep.1), channel_id=1, source_target_pairs={{0,8},{8,16},{16,24},{24,0},{1,9},{9,17},{17,25},{25,1},{2,10},{10... | collective-permute-start | bytes 147464 | tf_op jit(solution)/shard_map/ppermute | solution.py:409
  8.7 12.8 %collective-permute-start.4 = (f32[192,256]{1,0:T(8,128)S(1)}, f32[192,256]{1,0:T(8,128)S(1)}, u32[]{:S(2)}, u32[]{:S(2)}) collective-permute-start(f32[192,256]{1,0:T(8,128)S(1)} %pad_maximum_fusion.obs_ref), channel_id=1, source_target_pairs={{1,0},{2,1},{3,2},{4,3},{5,4},{6,5},{7,6},{9,8},{10,9},{11,10},{12... | collective-permute-start | bytes 589832 | tf_op jit(solution)/shard_map/ppermute | solution.py:414
  13.0 8.8 %collective-permute-start.6 = (f32[2,128]{1,0:T(2,128)S(1)}, f32[2,128]{1,0:T(2,128)S(1)}, u32[]{:S(2)}, u32[]{:S(2)}) collective-permute-start(f32[2,128]{1,0:T(2,128)S(1)} %slice_reduce_fusion.2), channel_id=1, source_target_pairs={{0,4},{1,5},{2,6},{3,7},{4,0},{5,1},{6,2},{7,3},{8,12},{9,13},{10,... | collective-permute-start | bytes 3080 | tf_op jit(solution)/shard_map/ppermute | solution.py:419
  15.3 6.4 %collective-permute-start.5 = (f32[2,128]{1,0:T(2,128)S(1)}, f32[2,128]{1,0:T(2,128)S(1)}, u32[]{:S(2)}, u32[]{:S(2)}) collective-permute-start(f32[2,128]{1,0:T(2,128)S(1)} %slice_reduce_fusion.2), channel_id=1, source_target_pairs={{0,2},{1,3},{2,0},{3,1},{4,6},{5,7},{6,4},{7,5},{8,10},{9,11},{10,... | collective-permute-start | bytes 3080 | tf_op jit(solution)/shard_map/ppermute | solution.py:419
  16.7 5.1 %collective-permute-start.3 = (f32[192,256]{1,0:T(8,128)S(1)}, f32[192,256]{1,0:T(8,128)S(1)}, u32[]{:S(2)}, u32[]{:S(2)}) collective-permute-start(f32[192,256]{1,0:T(8,128)S(1)} %pad_maximum_fusion.obs_ref), channel_id=1, source_target_pairs={{0,1},{1,2},{2,3},{3,4},{4,5},{5,6},{6,7},{8,9},{9,10},{10,11},{11... | collective-permute-start | bytes 589832 | tf_op jit(solution)/shard_map/ppermute | solution.py:414
  21.8 6.6 %collective-permute-start.7 = (f32[2,128]{1,0:T(2,128)S(1)}, f32[2,128]{1,0:T(2,128)S(1)}, u32[]{:S(2)}, u32[]{:S(2)}) collective-permute-start(f32[2,128]{1,0:T(2,128)S(1)} %add_add_fusion.refs_3_), channel_id=1, source_target_pairs={{0,7},{1,6},{2,5},{3,4},{4,3},{5,2},{6,1},{7,0},{8,15},{9,14},{10,... | collective-permute-start | bytes 3080 | tf_op jit(solution)/shard_map/ppermute | solution.py:419

commit v3 on v2

--- a/solution.py
+++ b/solution.py
@@ -198,7 +198,7 @@
 
 
 def analysis_kernel(
-    members, grams, sums_a, sums_b, column_ref, out_ref, u_ref, v_ref, t_ref, s_ref, m_ref, w_ref, mean_ref, o_refs, out_v, out_sem
+    members, grams, sums_a, sums_b, column_ref, out_ref, u_ref, v_ref, t_ref, s_ref, m_ref, w_ref, mean_ref, l_ref, o_refs, out_v, out_sem
 ):
     _, cols_east, cols_north, levels = out_v.shape
     offsets, pull_row, _ = pair_rows(members)
@@ -256,7 +256,7 @@
             acc_u = [gram(offsets[i] + SUB * b) for b in range(blocks - own)]
             at = sub == i % SUB
             acc_u[0] = acc_u[0] + jnp.where(at, prior, 0.0)
-            acc_v = [jnp.zeros((SUB, wide), F32) for _ in range(own)] + [jnp.where(at, 1.0, 0.0)]
+            acc_v = [jnp.zeros((SUB, wide), F32) for _ in range(own)] + [jnp.where(at, scale, 0.0)]
             for p in range(i):
                 row = p * members
                 factor = u_ref[row + i : row + i + 1, :]
@@ -272,17 +272,17 @@
 
     def put_rows(start, stop):
         most = (stop - 1) // SUB + 1
-        pulls = [gram(pull_row + SUB * b) for b in range(most)]
+        pulls = [gram(pull_row + SUB * b) * (1.0 / (members - 1)) for b in range(most)]
         mean_w = [mean_ref[SUB * b : SUB * (b + 1), :] for b in range(most)]
         for i in range(start, stop):
             count = i // SUB + 1
             rows = [v_ref[i * members + SUB * b : i * members + SUB * (b + 1), :] for b in range(count)]
             solved = functools.reduce(lambda x, y: x + y, [x * y for x, y in zip(rows, pulls)])
             solved = jnp.sum(solved, axis=0, keepdims=True)
-            shift = jnp.sum(functools.reduce(lambda x, y: x + y, rows), axis=0, keepdims=True) * (-scale / members)
+            shift = jnp.sum(functools.reduce(lambda x, y: x + y, rows), axis=0, keepdims=True) * (-1.0 / members)
             for b in range(count):
                 mean_w[b] = mean_w[b] + solved * rows[b]
-            rows = [x * scale + shift for x in rows]
+            rows = [x + shift for x in rows]
             put(i, rows + [jnp.broadcast_to(shift, (SUB, wide))] * (blocks - count))
         for b in range(most):
             mean_ref[SUB * b : SUB * (b + 1), :] = mean_w[b]
@@ -329,41 +329,45 @@
         second = jnp.where(lower_lane, turned, low)
         return [first, second[0 : members - fold, :]]
 
-    def apply(a, b, o_ref):
+    def prepare(a, b, slot):
         left = jnp.concatenate(matrix(a, b) + matrix(a, b + 1), axis=0).astype(BF16)
+        l_ref[slot, b // 2] = left
+
+    def apply(a, b, slot, o_ref):
         right = jnp.concatenate([column_ref[a, b], column_ref[a, b + 1]], axis=1)
         right = jnp.concatenate([right, blank, right, blank], axis=0)
-        both = jnp.dot(left, right, preferred_element_type=F32)
+        both = jnp.dot(l_ref[slot, b // 2], right, preferred_element_type=F32)
         o_ref[b * pitch_o : b * pitch_o + members, :] = both[:members, 0:levels]
         o_ref[(b + 1) * pitch_o : (b + 1) * pitch_o + members, :] = both[members:, levels:]
 
     def emit(a, k, o_ref):
         out_v[k, a] = o_ref[pl.ds(k, cols_north, stride=pitch_o), :].astype(BF16)
 
-    def step(a, to_ref, from_ref):
-        done = 0
-        for b in range(0, cols_north, 2):
-            if to_ref is not None:
-                apply(a, b, to_ref)
-            if from_ref is not None:
+    group = 4
+
+    def column_rows(t, carry):
+        for s in range(group):
+            a = group * t + s
+            done = 0
+            for b in range(0, cols_north, 2):
+                apply(a, b, s % 2, o_refs[s % 2])
+                prepare(jnp.minimum(a + 1, cols_east - 1), b, (s + 1) % 2)
                 upto = members * (b + 2) // cols_north
-                for k in range(done, upto):
-                    emit(a - 1, k, from_ref)
+                if s:
+                    for k in range(done, upto):
+                        emit(a - 1, k, o_refs[(s - 1) % 2])
                 done = upto
-        if from_ref is not None:
-            flush(a - 1).start()
-
-    even, odd = o_refs
-    step(0, even, None)
-
-    def column_rows(t, carry):
-        step(2 * t + 1, odd, even)
-        step(2 * t + 2, even, odd)
+            if s:
+                flush(a - 1).start()
+        a = group * t + group - 1
+        for k in range(members):
+            emit(a, k, o_refs[(group - 1) % 2])
+        flush(a).start()
         return carry
 
-    lax.fori_loop(0, cols_east // 2 - 1, column_rows, 0)
-    step(cols_east - 1, odd, even)
-    step(cols_east, None, odd)
+    for b in range(0, cols_north, 2):
+        prepare(0, b, 0)
+    lax.fori_loop(0, cols_east // group, column_rows, 0)
     for a in range(cols_east):
         flush(a).wait()
 
@@ -375,7 +379,7 @@
 
     def body(*refs):
         rest = refs[tables:]
-        analysis_kernel(members, refs[:tables], *rest[:11], rest[11:13], *rest[13:])
+        analysis_kernel(members, refs[:tables], *rest[:12], rest[12:14], *rest[14:])
 
     vmem = pl.BlockSpec(memory_space=pltpu.VMEM)
     hbm = pl.BlockSpec(memory_space=pltpu.HBM)
@@ -394,6 +398,7 @@
             pltpu.VMEM((count, LANES), F32),
             pltpu.VMEM((count // 2, 2 * LANES), BF16),
             pltpu.VMEM((members, 2 * LANES), F32),
+            pltpu.VMEM((2, cols_north // 2, 2 * members, LANES), BF16),
             pltpu.VMEM((cols_north * (members + 1), levels), F32),
             pltpu.VMEM((cols_north * (members + 1), levels), F32),
             pltpu.VMEM(shape, BF16),
@@ -409,14 +414,15 @@
     return lax.ppermute(value, axis, [(i, (i + step) % count) for i in range(count)])
 
 
-def slide(value, axis, step):
+def swap(value, axis, bits):
     count = lax.axis_size(axis)
-    return lax.ppermute(value, axis, [(i, i + step) for i in range(count) if 0 <= i + step < count])
-
-
-def swap(value, axis, bit):
+    return lax.ppermute(value, axis, [(i, i ^ bits) for i in range(count) if i ^ bits < count])
+
+
+def swap_beside(value, axis):
     count = lax.axis_size(axis)
-    return lax.ppermute(value, axis, [(i, i ^ bit) for i in range(count)])
+    pairs = [(i, ((i + 1) ^ 1) - 1) for i in range(count)]
+    return lax.ppermute(value, axis, [(i, j) for i, j in pairs if 0 <= j < count])
 
 
 def per_device(background, obs_perturb, innovation, obs_precision, obs_column, obs_count):
@@ -436,26 +442,32 @@
         name="prep",
     )(obs_count, *(pltpu.with_memory_space_constraint(x, pltpu.HBM) for x in inputs))
     steps = sorted({s % count_east for s in (-2, -1, 1, 2)} - {0})
-    around = [rotate(bundle, "gx", s) for s in steps]
-    columns = by_column(background)
+    if count_east == 4:
+        around = [swap(bundle, "gx", bits) for bits in (3, 2, 1)]
+    else:
+        around = [rotate(bundle, "gx", s) for s in steps]
+    *around, columns = lax.optimization_barrier((*around, by_column(background)))
     own = jnp.concatenate([bundle] + around, axis=0)
-    below = slide(own, "gy", 1)
-    above = slide(own, "gy", -1)
+    beside = swap_beside(own, "gy")
+    partner = swap(own, "gy", 1)
 
     def row_sum(bundles):
         each = bundles.reshape(-1, ROWS, slots)[:, members + 3 : members + 5, 0:LANES]
         return jnp.sum(each, axis=0)
 
+    table = functools.partial(gram_table, members=members, cols_east=cols_east, cols_north=cols_north)
     if len(steps) + 1 == count_east and count_north == 8:
-        mine = row_sum(own)
-        far = swap(mine, "gy", 2), swap(mine, "gy", 4)
-        beside = jnp.where(lax.axis_index("gy") % 2 == 0, row_sum(above), row_sum(below))
-        total = (mine + beside) + (far[0] + far[1])
-        other = swap(total, "gy", 7)
+        total = row_sum(own) + row_sum(partner)
+        own, total = lax.optimization_barrier((own, total))
+        total = total + swap(total, "gy", 2)
+        first = table(own)
+        partner, total = lax.optimization_barrier((partner, total))
+        other = swap(total, "gy", 4)
+        grams = [first, table(partner), table(beside)]
     else:
         total = lax.psum(bundle[members + 3 : members + 5, 0:LANES], ("gx", "gy"))
         other = jnp.zeros_like(total)
-    grams = [gram_table(x, members, cols_east, cols_north) for x in (own, below, above)]
+        grams = [table(x) for x in (own, partner, beside)]
     return analyse(grams, total, other, columns, members)
 
 

time: 37.9 us -> 34.2 us (0.902)
  the two profiles are of different devices: /device:TPU:1 before, /device:TPU:0 now
where the time goes in v3:
time: 34.2 us; the launch traced here: 34 us
  Pallas kernels  19.1 us (56%)
  starting transfers between devices  11.2 us (33%)
  waiting for transfers between devices  2.92 us (9%)
  between operations  0.76 us (2%)
    ppermute x6, starting transfers between devices, swap(): lax.ppermute(value, axis, [(i, i ^ bits) for i in range(count) if i ^ bit...  10.5 us
    pallas_call x1, Pallas kernels, analyse(): pl.pallas_call(body, out_shape=jax.ShapeDtypeStruct(shape, BF16), in_spec...  8.58 us
    pallas_call x3, Pallas kernels, gram_table(): pl.pallas_call(functools.partial(gram_kernel, members, cols_east, cols_no...  6.83 us
    ppermute x6, waiting for transfers between devices, swap(): lax.ppermute(value, axis, [(i, i ^ bits) for i in range(count) if i ^ bit...  2.92 us
    pallas_call x1, Pallas kernels, by_column(): pl.pallas_call(columns_kernel, out_shape=jax.ShapeDtypeStruct(shape, BF16...  2.76 us
    pallas_call x1, Pallas kernels, per_device(): pl.pallas_call(functools.partial(prep_kernel, cols_east, cols_north), out...  0.88 us
  transfers between devices with their start and end apart: 7, of which 2 were waited for; matrix products, arithmetic and copies ran while one was open for 0% of the time, Pallas kernels for 28%

profile of v3, /device:TPU:0, one launch (start us, length us, event | category | flops | bytes accessed | tf_op | source)
XLA Modules:
  0.0 34.0 jit_solution(4374596876086878972)
XLA Ops:
  0.7 0.9 %prep.1 = f32[48,256]{1,0:T(8,128)S(1)} custom-call(s32[1,1]{1,0:T(1,128)S(6)} %copy.7.count_ref, bf16[40,256]{1,0:T(8,128)(2,1)} %bitcast.8, f32[1,256]{1,0:T(1,128)} %bitcast.9, f32[1,256]{1,0:T(1,128)} %bitcast.10, s32[1,256]{1,0:T(1,128)} %bitcast.11), custom_call_target="tpu_custom_call" | custom-call | tf_op jit(solution)/shard_map/prep/pallas_call | solution.py:435
  1.5 3.0 %collective-permute-start.2 = (f32[48,256]{1,0:T(8,128)S(1)}, f32[48,256]{1,0:T(8,128)S(1)}, u32[]{:S(2)}, u32[]{:S(2)}) collective-permute-start(f32[48,256]{1,0:T(8,128)S(1)} %prep.1), channel_id=1, source_target_pairs={{0,8},{8,0},{16,24},{24,16},{1,9},{9,1},{17,25},{25,17},{2,10},{10... | collective-permute-start | bytes 147464 | tf_op jit(solution)/shard_map/ppermute | solution.py:419
  4.6 1.5 %collective-permute-start.1 = (f32[48,256]{1,0:T(8,128)S(1)}, f32[48,256]{1,0:T(8,128)S(1)}, u32[]{:S(2)}, u32[]{:S(2)}) collective-permute-start(f32[48,256]{1,0:T(8,128)S(1)} %prep.1), channel_id=1, source_target_pairs={{0,16},{8,24},{16,0},{24,8},{1,17},{9,25},{17,1},{25,9},{2,18},{10... | collective-permute-start | bytes 147464 | tf_op jit(solution)/shard_map/ppermute | solution.py:419
  6.1 0.0 collective-permute-start
  6.1 2.8 %columns.1.refs_5_ = bf16[16,32,48,128]{3,2,1,0:T(8,128)(2,1)S(1)} custom-call(bf16[40,16,32,128]{3,2,1,0:T(8,128)(2,1)} %state_ref.1), custom_call_target="tpu_custom_call" | custom-call | bytes 12582912 | tf_op jit(solution)/shard_map/columns/pallas_call | solution.py:183
  8.9 0.0 collective-permute-done.2
  8.9 0.0 collective-permute-done.1
  8.9 2.2 %collective-permute-done = f32[48,256]{1,0:T(8,128)S(1)} collective-permute-done((f32[48,256]{1,0:T(8,128)S(1)}, f32[48,256]{1,0:T(8,128)S(1)}, u32[]{:S(2)}, u32[]{:S(2)}) %collective-permute-start) | collective-permute-done | bytes 49184 | tf_op jit(solution)/shard_map/ppermute | solution.py:419
  11.1 0.1 collective-permute-start.3
  11.2 0.7 %collective-permute-start.5 = (f32[192,256]{1,0:T(8,128)S(1)}, f32[192,256]{1,0:T(8,128)S(1)}, u32[]{:S(2)}, u32[]{:S(2)}) collective-permute-start(f32[192,256]{1,0:T(8,128)S(1)} %pad_maximum_fusion.obs_ref), channel_id=1, source_target_pairs={{1,2},{2,1},{3,4},{4,3},{5,6},{6,5},{9,10},{10,9},{11,12},{12,11},... | collective-permute-start | bytes 589832 | tf_op jit(solution)/shard_map/ppermute | solution.py:425
  11.9 0.7 %collective-permute-done.3.obs_ref = f32[192,256]{1,0:T(8,128)S(1)} collective-permute-done((f32[192,256]{1,0:T(8,128)S(1)}, f32[192,256]{1,0:T(8,128)S(1)}, u32[]{:S(2)}, u32[]{:S(2)}) %collective-permute-start.3) | collective-permute-done | bytes 196640 | tf_op jit(solution)/shard_map/ppermute | solution.py:419
  12.6 2.7 %collective-permute-start.4 = (f32[2,128]{1,0:T(2,128)S(1)}, f32[2,128]{1,0:T(2,128)S(1)}, u32[]{:S(2)}, u32[]{:S(2)}) collective-permute-start(f32[2,128]{1,0:T(2,128)S(1)} %add.6), channel_id=1, source_target_pairs={{0,2},{1,3},{2,0},{3,1},{4,6},{5,7},{6,4},{7,5},{8,10},{9,11},{10,... | collective-permute-start | bytes 3080 | tf_op jit(solution)/shard_map/ppermute | solution.py:419
  15.3 2.3 %gram_table.3.refs_0_ = f32[1008,256]{1,0:T(8,128)S(1)} custom-call(f32[192,256]{1,0:T(8,128)S(1)} %pad_maximum_fusion.obs_ref), custom_call_target="tpu_custom_call" | custom-call | flops 1585446912 | bytes 2097152 | tf_op jit(solution)/shard_map/gram_table/pallas_call | solution.py:132
  17.6 0.0 collective-permute-done.5.obs_ref
  17.6 2.3 %gram_table.5.refs_2_ = f32[1008,256]{1,0:T(8,128)S(1)} custom-call(f32[192,256]{1,0:T(8,128)S(1)} %collective-permute-done.5.obs_ref), custom_call_target="tpu_custom_call" | custom-call | flops 1585446912 | bytes 2097152 | tf_op jit(solution)/shard_map/gram_table/pallas_call | solution.py:132
  19.9 0.0 collective-permute-done.4
  19.9 3.2 %collective-permute-start.6 = (f32[2,128]{1,0:T(2,128)S(1)}, f32[2,128]{1,0:T(2,128)S(1)}, u32[]{:S(2)}, u32[]{:S(2)}) collective-permute-start(f32[2,128]{1,0:T(2,128)S(1)} %add.7.refs_3_), channel_id=1, source_target_pairs={{0,4},{1,5},{2,6},{3,7},{4,0},{5,1},{6,2},{7,3},{8,12},{9,13},{10,... | collective-permute-start | bytes 3080 | tf_op jit(solution)/shard_map/ppermute | solution.py:419
  23.1 2.3 %gram_table.4.refs_1_ = f32[1008,256]{1,0:T(8,128)S(1)} custom-call(f32[192,256]{1,0:T(8,128)S(1)} %collective-permute-done.3.obs_ref), custom_call_target="tpu_custom_call" | custom-call | flops 1585446912 | bytes 2097152 | tf_op jit(solution)/shard_map/gram_table/pallas_call | solution.py:132
  25.4 0.0 collective-permute-done.6.refs_4_
  25.4 8.6 %analyse.1 = bf16[40,16,32,128]{3,2,1,0:T(8,128)(2,1)} custom-call(f32[1008,256]{1,0:T(8,128)S(1)} %gram_table.3.refs_0_, f32[1008,256]{1,0:T(8,128)S(1)} %gram_table.4.refs_1_, f32[1008,256]{1,0:T(8,128)S(1)} %gram_table.5.refs_2_, f32[2,128]{1,0:T(2,128)S(1)} %add.7.refs_3_, f32[2,128]{1,0:T(2,128)S(1)} %collective-permute-done.6.refs_4_, ...), custom_call_target="tpu_custom_call" | custom-call | tf_op jit(solution)/shard_map/analyse/pallas_call | solution.py:388
  (5 shorter events, 0.1 us)
Async XLA Ops:
  1.5 7.3 %collective-permute-start.2 = (f32[48,256]{1,0:T(8,128)S(1)}, f32[48,256]{1,0:T(8,128)S(1)}, u32[]{:S(2)}, u32[]{:S(2)}) collective-permute-start(f32[48,256]{1,0:T(8,128)S(1)} %prep.1), channel_id=1, source_target_pairs={{0,8},{8,0},{16,24},{24,16},{1,9},{9,1},{17,25},{25,17},{2,10},{10... | collective-permute-start | bytes 147464 | tf_op jit(solution)/shard_map/ppermute | solution.py:419
  4.6 4.3 %collective-permute-start.1 = (f32[48,256]{1,0:T(8,128)S(1)}, f32[48,256]{1,0:T(8,128)S(1)}, u32[]{:S(2)}, u32[]{:S(2)}) collective-permute-start(f32[48,256]{1,0:T(8,128)S(1)} %prep.1), channel_id=1, source_target_pairs={{0,16},{8,24},{16,0},{24,8},{1,17},{9,25},{17,1},{25,9},{2,18},{10... | collective-permute-start | bytes 147464 | tf_op jit(solution)/shard_map/ppermute | solution.py:419
  6.1 5.0 %collective-permute-start = (f32[48,256]{1,0:T(8,128)S(1)}, f32[48,256]{1,0:T(8,128)S(1)}, u32[]{:S(2)}, u32[]{:S(2)}) collective-permute-start(f32[48,256]{1,0:T(8,128)S(1)} %prep.1), channel_id=1, source_target_pairs={{0,24},{8,16},{16,8},{24,0},{1,25},{9,17},{17,9},{25,1},{2,26},{10... | collective-permute-start | bytes 147464 | tf_op jit(solution)/shard_map/ppermute | solution.py:419
  11.1 1.5 %collective-permute-start.3 = (f32[192,256]{1,0:T(8,128)S(1)}, f32[192,256]{1,0:T(8,128)S(1)}, u32[]{:S(2)}, u32[]{:S(2)}) collective-permute-start(f32[192,256]{1,0:T(8,128)S(1)} %pad_maximum_fusion.obs_ref), channel_id=1, source_target_pairs={{0,1},{1,0},{2,3},{3,2},{4,5},{5,4},{6,7},{7,6},{8,9},{9,8},{10,11... | collective-permute-start | bytes 589832 | tf_op jit(solution)/shard_map/ppermute | solution.py:419
  11.2 6.4 %collective-permute-start.5 = (f32[192,256]{1,0:T(8,128)S(1)}, f32[192,256]{1,0:T(8,128)S(1)}, u32[]{:S(2)}, u32[]{:S(2)}) collective-permute-start(f32[192,256]{1,0:T(8,128)S(1)} %pad_maximum_fusion.obs_ref), channel_id=1, source_target_pairs={{1,2},{2,1},{3,4},{4,3},{5,6},{6,5},{9,10},{10,9},{11,12},{12,11},... | collective-permute-start | bytes 589832 | tf_op jit(solution)/shard_map/ppermute | solution.py:425
  12.6 7.3 %collective-permute-start.4 = (f32[2,128]{1,0:T(2,128)S(1)}, f32[2,128]{1,0:T(2,128)S(1)}, u32[]{:S(2)}, u32[]{:S(2)}) collective-permute-start(f32[2,128]{1,0:T(2,128)S(1)} %add.6), channel_id=1, source_target_pairs={{0,2},{1,3},{2,0},{3,1},{4,6},{5,7},{6,4},{7,5},{8,10},{9,11},{10,... | collective-permute-start | bytes 3080 | tf_op jit(solution)/shard_map/ppermute | solution.py:419
  19.9 5.5 %collective-permute-start.6 = (f32[2,128]{1,0:T(2,128)S(1)}, f32[2,128]{1,0:T(2,128)S(1)}, u32[]{:S(2)}, u32[]{:S(2)}) collective-permute-start(f32[2,128]{1,0:T(2,128)S(1)} %add.7.refs_3_), channel_id=1, source_target_pairs={{0,4},{1,5},{2,6},{3,7},{4,0},{5,1},{6,2},{7,3},{8,12},{9,13},{10,... | collective-permute-start | bytes 3080 | tf_op jit(solution)/shard_map/ppermute | solution.py:419

commit v4 on v3

--- a/solution.py
+++ b/solution.py
@@ -59,9 +59,10 @@
     out_ref[members:ROWS, :] = rest
 
 
-def gram_kernel(members, cols_east, cols_north, obs_ref, out_ref, lhs_hi, lhs_lo, rhs_hi, rhs_lo):
-    tiles = obs_ref.shape[0] // ROWS
-    slots = obs_ref.shape[1]
+def gram_kernel(members, cols_east, cols_north, obs_refs, out_ref, lhs_hi, lhs_lo, rhs_hi, rhs_lo):
+    each = obs_refs[0].shape[0] // ROWS
+    tiles = each * len(obs_refs)
+    slots = obs_refs[0].shape[1]
     offsets, pull_row, total = pair_rows(members)
     regions_north = cols_north // SPAN
     deep = regions_north // 2 + 2
@@ -83,7 +84,7 @@
     centre_north = centre_north * inv_radius
 
     def build(t):
-        base = t * ROWS
+        obs_ref, base = obs_refs[t // each], t % each * ROWS
         place = jnp.transpose(obs_ref[base + members : base + ROWS, :])
         east, north = place[:, 1:2], place[:, 2:3] * inv_radius
         away = jnp.abs(east - centre_east)
@@ -110,29 +111,37 @@
         lhs_hi[pull_row:total, span] = hi
         lhs_lo[pull_row:total, span] = (table - hi.astype(F32)).astype(BF16)
 
-    def multiply(t):
-        span = slice(t * slots, (t + 1) * slots)
+    def multiply(start, stop):
+        span = slice(start * slots, stop * slots)
         left = jnp.concatenate([lhs_hi[:, span], lhs_lo[:, span], lhs_hi[:, span]], axis=1)
         right = jnp.concatenate([rhs_hi[span, :], rhs_hi[span, :], rhs_lo[span, :]], axis=0)
         return jnp.dot(left, right, preferred_element_type=F32)
 
+    edges = [0, *range(1, tiles, 2), tiles]
+    parts = list(zip(edges, edges[1:]))
     build(0)
-    for t in range(tiles):
-        if t + 1 < tiles:
-            build(t + 1)
-        if t == 0:
-            out_ref[...] = multiply(t)
+    for n, (start, stop) in enumerate(parts):
+        if n + 1 < len(parts):
+            for t in range(*parts[n + 1]):
+                build(t)
+        if n == 0:
+            out_ref[...] = multiply(start, stop)
         else:
-            out_ref[...] += multiply(t)
-
-
-def gram_table(bundles, members, cols_east, cols_north):
+            out_ref[...] += multiply(start, stop)
+
+
+def gram_table(*bundles, members, cols_east, cols_north):
     total = pair_rows(members)[2]
-    deep = bundles.shape[0] // ROWS * bundles.shape[1]
+    deep = sum(x.shape[0] // ROWS * x.shape[1] for x in bundles)
+    count = len(bundles)
+
+    def body(*refs):
+        gram_kernel(members, cols_east, cols_north, refs[:count], *refs[count:])
+
     return pl.pallas_call(
-        functools.partial(gram_kernel, members, cols_east, cols_north),
+        body,
         out_shape=jax.ShapeDtypeStruct((total, 2 * LANES), F32),
-        in_specs=[pl.BlockSpec(memory_space=pltpu.VMEM)],
+        in_specs=[pl.BlockSpec(memory_space=pltpu.VMEM)] * count,
         out_specs=pl.BlockSpec(memory_space=pltpu.VMEM),
         scratch_shapes=[
             pltpu.VMEM((total, deep), BF16),
@@ -140,10 +149,10 @@
             pltpu.VMEM((deep, 2 * LANES), BF16),
             pltpu.VMEM((deep, 2 * LANES), BF16),
         ],
-        compiler_params=pltpu.CompilerParams(vmem_limit_bytes=16 << 20),
+        compiler_params=pltpu.CompilerParams(vmem_limit_bytes=(12 << 20) * count),
         cost_estimate=pl.CostEstimate(flops=6 * total * deep * 2 * LANES, bytes_accessed=1 << 21, transcendentals=0),
         name="gram_table",
-    )(bundles)
+    )(*bundles)
 
 
 def columns_kernel(state_ref, out_ref, state_v, even_ref, odd_ref, in_sem):
@@ -198,7 +207,7 @@
 
 
 def analysis_kernel(
-    members, grams, sums_a, sums_b, column_ref, out_ref, u_ref, v_ref, t_ref, s_ref, m_ref, w_ref, mean_ref, l_ref, o_refs, out_v, out_sem
+    members, grams, sums, column_ref, out_ref, u_ref, v_ref, t_ref, s_ref, m_ref, w_ref, mean_ref, l_ref, o_refs, out_v, out_sem
 ):
     _, cols_east, cols_north, levels = out_v.shape
     offsets, pull_row, _ = pair_rows(members)
@@ -224,7 +233,7 @@
     w_ref[:, 0:LANES] = hats
     w_ref[:, LANES:wide] = hats
 
-    total = sums_a[...] + sums_b[...]
+    total = functools.reduce(lambda x, y: x + y, [x[...] for x in sums])
     prior = (members - 1) / (total[0:1, 0:1] / total[1:2, 0:1])
     sub = lax.broadcasted_iota(jnp.int32, (SUB, wide), 0)
     gap = jnp.zeros((SLOT - ROWS, wide), BF16)
@@ -372,14 +381,14 @@
         flush(a).wait()
 
 
-def analyse(grams, sums_a, sums_b, columns, members):
+def analyse(grams, sums, columns, members):
     cols_east, cols_north, _, levels = columns.shape
     count = cols_east * cols_north
-    tables = len(grams)
+    tables, most = len(grams), len(grams) + len(sums)
 
     def body(*refs):
-        rest = refs[tables:]
-        analysis_kernel(members, refs[:tables], *rest[:12], rest[12:14], *rest[14:])
+        rest = refs[most:]
+        analysis_kernel(members, refs[:tables], refs[tables:most], *rest[:10], rest[10:12], *rest[12:])
 
     vmem = pl.BlockSpec(memory_space=pltpu.VMEM)
     hbm = pl.BlockSpec(memory_space=pltpu.HBM)
@@ -388,7 +397,7 @@
     return pl.pallas_call(
         body,
         out_shape=jax.ShapeDtypeStruct(shape, BF16),
-        in_specs=[vmem] * (tables + 3),
+        in_specs=[vmem] * (most + 1),
         out_specs=hbm,
         scratch_shapes=[
             pltpu.VMEM((members * members, 2 * LANES), F32),
@@ -406,7 +415,7 @@
         ],
         compiler_params=pltpu.CompilerParams(vmem_limit_bytes=30 << 20),
         name="analyse",
-    )(*grams, sums_a, sums_b, columns)
+    )(*grams, *sums, columns)
 
 
 def rotate(value, axis, step):
@@ -443,7 +452,7 @@
     )(obs_count, *(pltpu.with_memory_space_constraint(x, pltpu.HBM) for x in inputs))
     steps = sorted({s % count_east for s in (-2, -1, 1, 2)} - {0})
     if count_east == 4:
-        around = [swap(bundle, "gx", bits) for bits in (3, 2, 1)]
+        around = [swap(bundle, "gx", bits) for bits in (1, 2, 3)]
     else:
         around = [rotate(bundle, "gx", s) for s in steps]
     *around, columns = lax.optimization_barrier((*around, by_column(background)))
@@ -457,18 +466,13 @@
 
     table = functools.partial(gram_table, members=members, cols_east=cols_east, cols_north=cols_north)
     if len(steps) + 1 == count_east and count_north == 8:
-        total = row_sum(own) + row_sum(partner)
-        own, total = lax.optimization_barrier((own, total))
-        total = total + swap(total, "gy", 2)
-        first = table(own)
-        partner, total = lax.optimization_barrier((partner, total))
-        other = swap(total, "gy", 4)
-        grams = [first, table(partner), table(beside)]
+        pair = row_sum(own) + row_sum(partner)
+        own, pair = lax.optimization_barrier((own, pair))
+        sums = [pair] + [swap(pair, "gy", bits) for bits in (2, 4, 6)]
     else:
-        total = lax.psum(bundle[members + 3 : members + 5, 0:LANES], ("gx", "gy"))
-        other = jnp.zeros_like(total)
-        grams = [table(x) for x in (own, partner, beside)]
-    return analyse(grams, total, other, columns, members)
+        sums = [lax.psum(bundle[members + 3 : members + 5, 0:LANES], ("gx", "gy"))]
+    grams = [table(own), table(partner, beside)]
+    return analyse(grams, sums, columns, members)
 
 
 def solution(mesh):

time: 34.2 us -> 32.3 us (0.944)
  waiting for transfers between devices: 2.92 us -> 1.91 us
  Pallas kernels: 19.1 us -> 18.5 us
  starting transfers between devices: 11.2 us -> 10.7 us
    ppermute x6 -> x7, waiting for transfers between devices: 2.92 us -> 1.91 us  [swap(): lax.ppermute(value, axis, [(i, i ^ bits) for i in range(count) if i ^ bit...]
    ppermute x6 -> x7, starting transfers between devices: 10.5 us -> 10.1 us  [swap(): lax.ppermute(value, axis, [(i, i ^ bits) for i in range(count) if i ^ bit...]
    pallas_call x3 -> x2, Pallas kernels: 6.83 us -> 6.38 us  [gram_table(): pl.pallas_call(body, out_shape=jax.ShapeDtypeStruct((total, 2 * LANES), F...]
  transfers between devices with their start and end apart: 7 -> 8, of which waited for: 2 -> 3; matrix products, arithmetic and copies ran while one was open for 0% -> 0% of each run, Pallas kernels for 28% -> 29%
where the time goes in v4:
time: 32.3 us; the launch traced here: 32 us
  Pallas kernels  18.5 us (57%)
  starting transfers between devices  10.7 us (33%)
  waiting for transfers between devices  1.91 us (6%)
  between operations  0.74 us (2%)
    ppermute x7, starting transfers between devices, swap(): lax.ppermute(value, axis, [(i, i ^ bits) for i in range(count) if i ^ bit...  10.1 us
    pallas_call x1, Pallas kernels, analyse(): pl.pallas_call(body, out_shape=jax.ShapeDtypeStruct(shape, BF16), in_spec...  8.49 us
    pallas_call x2, Pallas kernels, gram_table(): pl.pallas_call(body, out_shape=jax.ShapeDtypeStruct((total, 2 * LANES), F...  6.38 us
    pallas_call x1, Pallas kernels, by_column(): pl.pallas_call(columns_kernel, out_shape=jax.ShapeDtypeStruct(shape, BF16...  2.76 us
    ppermute x7, waiting for transfers between devices, swap(): lax.ppermute(value, axis, [(i, i ^ bits) for i in range(count) if i ^ bit...  1.91 us
    pallas_call x1, Pallas kernels, per_device(): pl.pallas_call(functools.partial(prep_kernel, cols_east, cols_north), out...  0.88 us
    ppermute x1, starting transfers between devices, swap_beside(): lax.ppermute(value, axis, [(i, j) for i, j in pairs if 0 <= j < count])  0.67 us
  transfers between devices with their start and end apart: 8, of which 3 were waited for; matrix products, arithmetic and copies ran while one was open for 0% of the time, Pallas kernels for 29%

profile of v4, /device:TPU:0, one launch (start us, length us, event | category | flops | bytes accessed | tf_op | source)
XLA Modules:
  0.0 32.0 jit_solution(14554217410805659781)
XLA Ops:
  0.7 0.9 %prep.1 = f32[48,256]{1,0:T(8,128)S(1)} custom-call(s32[1,1]{1,0:T(1,128)S(6)} %copy.7.count_ref, bf16[40,256]{1,0:T(8,128)(2,1)} %bitcast.8, f32[1,256]{1,0:T(1,128)} %bitcast.9, f32[1,256]{1,0:T(1,128)} %bitcast.10, s32[1,256]{1,0:T(1,128)} %bitcast.11), custom_call_target="tpu_custom_call" | custom-call | tf_op jit(solution)/shard_map/prep/pallas_call | solution.py:444
  1.5 4.0 %collective-permute-start.2 = (f32[48,256]{1,0:T(8,128)S(1)}, f32[48,256]{1,0:T(8,128)S(1)}, u32[]{:S(2)}, u32[]{:S(2)}) collective-permute-start(f32[48,256]{1,0:T(8,128)S(1)} %prep.1), channel_id=1, source_target_pairs={{0,24},{8,16},{16,8},{24,0},{1,25},{9,17},{17,9},{25,1},{2,26},{10... | collective-permute-start | bytes 147464 | tf_op jit(solution)/shard_map/ppermute | solution.py:428
  5.5 0.5 %collective-permute-start.1 = (f32[48,256]{1,0:T(8,128)S(1)}, f32[48,256]{1,0:T(8,128)S(1)}, u32[]{:S(2)}, u32[]{:S(2)}) collective-permute-start(f32[48,256]{1,0:T(8,128)S(1)} %prep.1), channel_id=1, source_target_pairs={{0,16},{8,24},{16,0},{24,8},{1,17},{9,25},{17,1},{25,9},{2,18},{10... | collective-permute-start | bytes 147464 | tf_op jit(solution)/shard_map/ppermute | solution.py:428
  6.0 0.1 collective-permute-start
  6.2 2.8 %columns.1.refs_6_ = bf16[16,32,48,128]{3,2,1,0:T(8,128)(2,1)S(1)} custom-call(bf16[40,16,32,128]{3,2,1,0:T(8,128)(2,1)} %state_ref.1), custom_call_target="tpu_custom_call" | custom-call | bytes 12582912 | tf_op jit(solution)/shard_map/columns/pallas_call | solution.py:192
  8.9 0.0 collective-permute-done.2
  9.0 0.7 %collective-permute-done.1 = f32[48,256]{1,0:T(8,128)S(1)} collective-permute-done((f32[48,256]{1,0:T(8,128)S(1)}, f32[48,256]{1,0:T(8,128)S(1)}, u32[]{:S(2)}, u32[]{:S(2)}) %collective-permute-start.1) | collective-permute-done | bytes 49184 | tf_op jit(solution)/shard_map/ppermute | solution.py:428
  9.6 0.5 %collective-permute-done = f32[48,256]{1,0:T(8,128)S(1)} collective-permute-done((f32[48,256]{1,0:T(8,128)S(1)}, f32[48,256]{1,0:T(8,128)S(1)}, u32[]{:S(2)}, u32[]{:S(2)}) %collective-permute-start) | collective-permute-done | bytes 49184 | tf_op jit(solution)/shard_map/ppermute | solution.py:428
  10.1 0.1 collective-permute-start.3
  10.2 0.7 %collective-permute-start.4 = (f32[192,256]{1,0:T(8,128)S(1)}, f32[192,256]{1,0:T(8,128)S(1)}, u32[]{:S(2)}, u32[]{:S(2)}) collective-permute-start(f32[192,256]{1,0:T(8,128)S(1)} %pad_maximum_fusion.refs_0_), channel_id=1, source_target_pairs={{1,2},{2,1},{3,4},{4,3},{5,6},{6,5},{9,10},{10,9},{11,12},{12,11},... | collective-permute-start | bytes 589832 | tf_op jit(solution)/shard_map/ppermute | solution.py:434
  10.9 0.7 %collective-permute-done.3.refs_0_ = f32[192,256]{1,0:T(8,128)S(1)} collective-permute-done((f32[192,256]{1,0:T(8,128)S(1)}, f32[192,256]{1,0:T(8,128)S(1)}, u32[]{:S(2)}, u32[]{:S(2)}) %collective-permute-start.3) | collective-permute-done | bytes 196640 | tf_op jit(solution)/shard_map/ppermute | solution.py:428
  11.7 4.7 %collective-permute-start.7 = (f32[2,128]{1,0:T(2,128)S(1)}, f32[2,128]{1,0:T(2,128)S(1)}, u32[]{:S(2)}, u32[]{:S(2)}) collective-permute-start(f32[2,128]{1,0:T(2,128)S(1)} %add.3.refs_2_), channel_id=1, source_target_pairs={{0,6},{1,7},{2,4},{3,5},{4,2},{5,3},{6,0},{7,1},{8,14},{9,15},{10,... | collective-permute-start | bytes 3080 | tf_op jit(solution)/shard_map/ppermute | solution.py:428
  16.4 0.0 collective-permute-start.6
  16.4 0.6 %collective-permute-start.5 = (f32[2,128]{1,0:T(2,128)S(1)}, f32[2,128]{1,0:T(2,128)S(1)}, u32[]{:S(2)}, u32[]{:S(2)}) collective-permute-start(f32[2,128]{1,0:T(2,128)S(1)} %add.3.refs_2_), channel_id=1, source_target_pairs={{0,2},{1,3},{2,0},{3,1},{4,6},{5,7},{6,4},{7,5},{8,10},{9,11},{10,... | collective-permute-start | bytes 3080 | tf_op jit(solution)/shard_map/ppermute | solution.py:428
  17.0 0.0 collective-permute-done.4.refs_1_
  17.0 4.1 %gram_table.3.refs_1_ = f32[1008,256]{1,0:T(8,128)S(1)} custom-call(f32[192,256]{1,0:T(8,128)S(1)} %collective-permute-done.3.refs_0_, f32[192,256]{1,0:T(8,128)S(1)} %collective-permute-done.4.refs_1_), custom_call_target="tpu_custom_call" | custom-call | flops 3170893824 | bytes 2097152 | tf_op jit(solution)/shard_map/gram_table/pallas_call | solution.py:141
  21.1 2.3 %gram_table.2.refs_0_ = f32[1008,256]{1,0:T(8,128)S(1)} custom-call(f32[192,256]{1,0:T(8,128)S(1)} %pad_maximum_fusion.refs_0_), custom_call_target="tpu_custom_call" | custom-call | flops 1585446912 | bytes 2097152 | tf_op jit(solution)/shard_map/gram_table/pallas_call | solution.py:141
  23.4 0.0 collective-permute-done.7.refs_5_
  23.4 0.0 collective-permute-done.6.refs_4_
  23.5 0.0 collective-permute-done.5.refs_3_
  23.5 8.5 %analyse.1 = bf16[40,16,32,128]{3,2,1,0:T(8,128)(2,1)} custom-call(f32[1008,256]{1,0:T(8,128)S(1)} %gram_table.2.refs_0_, f32[1008,256]{1,0:T(8,128)S(1)} %gram_table.3.refs_1_, f32[2,128]{1,0:T(2,128)S(1)} %add.3.refs_2_, f32[2,128]{1,0:T(2,128)S(1)} %collective-permute-done.5.refs_3_, f32[2,128]{1,0:T(2,128)S(1)} %collective-permute-done.6.refs_4_, ...), custom_call_target="tpu_custom_call" | custom-call | tf_op jit(solution)/shard_map/analyse/pallas_call | solution.py:397
  (4 shorter events, 0.0 us)
Async XLA Ops:
  1.5 7.4 %collective-permute-start.2 = (f32[48,256]{1,0:T(8,128)S(1)}, f32[48,256]{1,0:T(8,128)S(1)}, u32[]{:S(2)}, u32[]{:S(2)}) collective-permute-start(f32[48,256]{1,0:T(8,128)S(1)} %prep.1), channel_id=1, source_target_pairs={{0,24},{8,16},{16,8},{24,0},{1,25},{9,17},{17,9},{25,1},{2,26},{10... | collective-permute-start | bytes 147464 | tf_op jit(solution)/shard_map/ppermute | solution.py:428
  5.5 4.1 %collective-permute-start.1 = (f32[48,256]{1,0:T(8,128)S(1)}, f32[48,256]{1,0:T(8,128)S(1)}, u32[]{:S(2)}, u32[]{:S(2)}) collective-permute-start(f32[48,256]{1,0:T(8,128)S(1)} %prep.1), channel_id=1, source_target_pairs={{0,16},{8,24},{16,0},{24,8},{1,17},{9,25},{17,1},{25,9},{2,18},{10... | collective-permute-start | bytes 147464 | tf_op jit(solution)/shard_map/ppermute | solution.py:428
  6.0 4.1 %collective-permute-start = (f32[48,256]{1,0:T(8,128)S(1)}, f32[48,256]{1,0:T(8,128)S(1)}, u32[]{:S(2)}, u32[]{:S(2)}) collective-permute-start(f32[48,256]{1,0:T(8,128)S(1)} %prep.1), channel_id=1, source_target_pairs={{0,8},{8,0},{16,24},{24,16},{1,9},{9,1},{17,25},{25,17},{2,10},{10... | collective-permute-start | bytes 147464 | tf_op jit(solution)/shard_map/ppermute | solution.py:428
  10.1 1.5 %collective-permute-start.3 = (f32[192,256]{1,0:T(8,128)S(1)}, f32[192,256]{1,0:T(8,128)S(1)}, u32[]{:S(2)}, u32[]{:S(2)}) collective-permute-start(f32[192,256]{1,0:T(8,128)S(1)} %pad_maximum_fusion.refs_0_), channel_id=1, source_target_pairs={{0,1},{1,0},{2,3},{3,2},{4,5},{5,4},{6,7},{7,6},{8,9},{9,8},{10,11... | collective-permute-start | bytes 589832 | tf_op jit(solution)/shard_map/ppermute | solution.py:428
  10.2 6.8 %collective-permute-start.4 = (f32[192,256]{1,0:T(8,128)S(1)}, f32[192,256]{1,0:T(8,128)S(1)}, u32[]{:S(2)}, u32[]{:S(2)}) collective-permute-start(f32[192,256]{1,0:T(8,128)S(1)} %pad_maximum_fusion.refs_0_), channel_id=1, source_target_pairs={{1,2},{2,1},{3,4},{4,3},{5,6},{6,5},{9,10},{10,9},{11,12},{12,11},... | collective-permute-start | bytes 589832 | tf_op jit(solution)/shard_map/ppermute | solution.py:434
  11.7 11.8 %collective-permute-start.7 = (f32[2,128]{1,0:T(2,128)S(1)}, f32[2,128]{1,0:T(2,128)S(1)}, u32[]{:S(2)}, u32[]{:S(2)}) collective-permute-start(f32[2,128]{1,0:T(2,128)S(1)} %add.3.refs_2_), channel_id=1, source_target_pairs={{0,6},{1,7},{2,4},{3,5},{4,2},{5,3},{6,0},{7,1},{8,14},{9,15},{10,... | collective-permute-start | bytes 3080 | tf_op jit(solution)/shard_map/ppermute | solution.py:428
  16.4 7.1 %collective-permute-start.6 = (f32[2,128]{1,0:T(2,128)S(1)}, f32[2,128]{1,0:T(2,128)S(1)}, u32[]{:S(2)}, u32[]{:S(2)}) collective-permute-start(f32[2,128]{1,0:T(2,128)S(1)} %add.3.refs_2_), channel_id=1, source_target_pairs={{0,4},{1,5},{2,6},{3,7},{4,0},{5,1},{6,2},{7,3},{8,12},{9,13},{10,... | collective-permute-start | bytes 3080 | tf_op jit(solution)/shard_map/ppermute | solution.py:428
  16.4 7.1 %collective-permute-start.5 = (f32[2,128]{1,0:T(2,128)S(1)}, f32[2,128]{1,0:T(2,128)S(1)}, u32[]{:S(2)}, u32[]{:S(2)}) collective-permute-start(f32[2,128]{1,0:T(2,128)S(1)} %add.3.refs_2_), channel_id=1, source_target_pairs={{0,2},{1,3},{2,0},{3,1},{4,6},{5,7},{6,4},{7,5},{8,10},{9,11},{10,... | collective-permute-start | bytes 3080 | tf_op jit(solution)/shard_map/ppermute | solution.py:428

commit v5 on v4

--- a/solution.py
+++ b/solution.py
@@ -117,7 +117,7 @@
         right = jnp.concatenate([rhs_hi[span, :], rhs_hi[span, :], rhs_lo[span, :]], axis=0)
         return jnp.dot(left, right, preferred_element_type=F32)
 
-    edges = [0, *range(1, tiles, 2), tiles]
+    edges = [0, *range(1, tiles, 2 if tiles > each else 3), tiles]
     parts = list(zip(edges, edges[1:]))
     build(0)
     for n, (start, stop) in enumerate(parts):
@@ -352,7 +352,7 @@
     def emit(a, k, o_ref):
         out_v[k, a] = o_ref[pl.ds(k, cols_north, stride=pitch_o), :].astype(BF16)
 
-    group = 4
+    group = 8
 
     def column_rows(t, carry):
         for s in range(group):

time: 32.3 us -> 32.1 us (level)
  no operation moved by 1% of the time
where the time goes in v5:
time: 32.1 us; the launch traced here: 31.8 us
  Pallas kernels  18.3 us (57%)
  starting transfers between devices  10.7 us (33%)
  waiting for transfers between devices  1.91 us (6%)
  between operations  0.74 us (2%)
    ppermute x7, starting transfers between devices, swap(): lax.ppermute(value, axis, [(i, i ^ bits) for i in range(count) if i ^ bit...  10.1 us
    pallas_call x1, Pallas kernels, analyse(): pl.pallas_call(body, out_shape=jax.ShapeDtypeStruct(shape, BF16), in_spec...  8.31 us
    pallas_call x2, Pallas kernels, gram_table(): pl.pallas_call(body, out_shape=jax.ShapeDtypeStruct((total, 2 * LANES), F...  6.36 us
    pallas_call x1, Pallas kernels, by_column(): pl.pallas_call(columns_kernel, out_shape=jax.ShapeDtypeStruct(shape, BF16...  2.76 us
    ppermute x7, waiting for transfers between devices, swap(): lax.ppermute(value, axis, [(i, i ^ bits) for i in range(count) if i ^ bit...  1.91 us
    pallas_call x1, Pallas kernels, per_device(): pl.pallas_call(functools.partial(prep_kernel, cols_east, cols_north), out...  0.88 us
    ppermute x1, starting transfers between devices, swap_beside(): lax.ppermute(value, axis, [(i, j) for i, j in pairs if 0 <= j < count])  0.67 us
  transfers between devices with their start and end apart: 8, of which 3 were waited for; matrix products, arithmetic and copies ran while one was open for 0% of the time, Pallas kernels for 29%

profile of v5, /device:TPU:0, one launch (start us, length us, event | category | flops | bytes accessed | tf_op | source)
XLA Modules:
  0.0 31.8 jit_solution(6067905055486412028)
XLA Ops:
  0.7 0.9 %prep.1 = f32[48,256]{1,0:T(8,128)S(1)} custom-call(s32[1,1]{1,0:T(1,128)S(6)} %copy.7.count_ref, bf16[40,256]{1,0:T(8,128)(2,1)} %bitcast.8, f32[1,256]{1,0:T(1,128)} %bitcast.9, f32[1,256]{1,0:T(1,128)} %bitcast.10, s32[1,256]{1,0:T(1,128)} %bitcast.11), custom_call_target="tpu_custom_call" | custom-call | tf_op jit(solution)/shard_map/prep/pallas_call | solution.py:444
  1.5 4.0 %collective-permute-start.2 = (f32[48,256]{1,0:T(8,128)S(1)}, f32[48,256]{1,0:T(8,128)S(1)}, u32[]{:S(2)}, u32[]{:S(2)}) collective-permute-start(f32[48,256]{1,0:T(8,128)S(1)} %prep.1), channel_id=1, source_target_pairs={{0,24},{8,16},{16,8},{24,0},{1,25},{9,17},{17,9},{25,1},{2,26},{10... | collective-permute-start | bytes 147464 | tf_op jit(solution)/shard_map/ppermute | solution.py:428
  5.5 0.5 %collective-permute-start.1 = (f32[48,256]{1,0:T(8,128)S(1)}, f32[48,256]{1,0:T(8,128)S(1)}, u32[]{:S(2)}, u32[]{:S(2)}) collective-permute-start(f32[48,256]{1,0:T(8,128)S(1)} %prep.1), channel_id=1, source_target_pairs={{0,16},{8,24},{16,0},{24,8},{1,17},{9,25},{17,1},{25,9},{2,18},{10... | collective-permute-start | bytes 147464 | tf_op jit(solution)/shard_map/ppermute | solution.py:428
  6.0 0.1 collective-permute-start
  6.2 2.8 %columns.1.refs_6_ = bf16[16,32,48,128]{3,2,1,0:T(8,128)(2,1)S(1)} custom-call(bf16[40,16,32,128]{3,2,1,0:T(8,128)(2,1)} %state_ref.1), custom_call_target="tpu_custom_call" | custom-call | bytes 12582912 | tf_op jit(solution)/shard_map/columns/pallas_call | solution.py:192
  8.9 0.0 collective-permute-done.2
  9.0 0.7 %collective-permute-done.1 = f32[48,256]{1,0:T(8,128)S(1)} collective-permute-done((f32[48,256]{1,0:T(8,128)S(1)}, f32[48,256]{1,0:T(8,128)S(1)}, u32[]{:S(2)}, u32[]{:S(2)}) %collective-permute-start.1) | collective-permute-done | bytes 49184 | tf_op jit(solution)/shard_map/ppermute | solution.py:428
  9.6 0.5 %collective-permute-done = f32[48,256]{1,0:T(8,128)S(1)} collective-permute-done((f32[48,256]{1,0:T(8,128)S(1)}, f32[48,256]{1,0:T(8,128)S(1)}, u32[]{:S(2)}, u32[]{:S(2)}) %collective-permute-start) | collective-permute-done | bytes 49184 | tf_op jit(solution)/shard_map/ppermute | solution.py:428
  10.1 0.1 collective-permute-start.3
  10.2 0.7 %collective-permute-start.4 = (f32[192,256]{1,0:T(8,128)S(1)}, f32[192,256]{1,0:T(8,128)S(1)}, u32[]{:S(2)}, u32[]{:S(2)}) collective-permute-start(f32[192,256]{1,0:T(8,128)S(1)} %pad_maximum_fusion.refs_0_), channel_id=1, source_target_pairs={{1,2},{2,1},{3,4},{4,3},{5,6},{6,5},{9,10},{10,9},{11,12},{12,11},... | collective-permute-start | bytes 589832 | tf_op jit(solution)/shard_map/ppermute | solution.py:434
  10.9 0.7 %collective-permute-done.3.refs_0_ = f32[192,256]{1,0:T(8,128)S(1)} collective-permute-done((f32[192,256]{1,0:T(8,128)S(1)}, f32[192,256]{1,0:T(8,128)S(1)}, u32[]{:S(2)}, u32[]{:S(2)}) %collective-permute-start.3) | collective-permute-done | bytes 196640 | tf_op jit(solution)/shard_map/ppermute | solution.py:428
  11.7 4.7 %collective-permute-start.7 = (f32[2,128]{1,0:T(2,128)S(1)}, f32[2,128]{1,0:T(2,128)S(1)}, u32[]{:S(2)}, u32[]{:S(2)}) collective-permute-start(f32[2,128]{1,0:T(2,128)S(1)} %add.3.refs_2_), channel_id=1, source_target_pairs={{0,6},{1,7},{2,4},{3,5},{4,2},{5,3},{6,0},{7,1},{8,14},{9,15},{10,... | collective-permute-start | bytes 3080 | tf_op jit(solution)/shard_map/ppermute | solution.py:428
  16.4 0.0 collective-permute-start.6
  16.4 0.6 %collective-permute-start.5 = (f32[2,128]{1,0:T(2,128)S(1)}, f32[2,128]{1,0:T(2,128)S(1)}, u32[]{:S(2)}, u32[]{:S(2)}) collective-permute-start(f32[2,128]{1,0:T(2,128)S(1)} %add.3.refs_2_), channel_id=1, source_target_pairs={{0,2},{1,3},{2,0},{3,1},{4,6},{5,7},{6,4},{7,5},{8,10},{9,11},{10,... | collective-permute-start | bytes 3080 | tf_op jit(solution)/shard_map/ppermute | solution.py:428
  17.0 0.0 collective-permute-done.4.refs_1_
  17.0 4.1 %gram_table.3.refs_1_ = f32[1008,256]{1,0:T(8,128)S(1)} custom-call(f32[192,256]{1,0:T(8,128)S(1)} %collective-permute-done.3.refs_0_, f32[192,256]{1,0:T(8,128)S(1)} %collective-permute-done.4.refs_1_), custom_call_target="tpu_custom_call" | custom-call | flops 3170893824 | bytes 2097152 | tf_op jit(solution)/shard_map/gram_table/pallas_call | solution.py:141
  21.1 2.3 %gram_table.2.refs_0_ = f32[1008,256]{1,0:T(8,128)S(1)} custom-call(f32[192,256]{1,0:T(8,128)S(1)} %pad_maximum_fusion.refs_0_), custom_call_target="tpu_custom_call" | custom-call | flops 1585446912 | bytes 2097152 | tf_op jit(solution)/shard_map/gram_table/pallas_call | solution.py:141
  23.4 0.0 collective-permute-done.7.refs_5_
  23.4 0.0 collective-permute-done.6.refs_4_
  23.4 0.0 collective-permute-done.5.refs_3_
  23.5 8.3 %analyse.1 = bf16[40,16,32,128]{3,2,1,0:T(8,128)(2,1)} custom-call(f32[1008,256]{1,0:T(8,128)S(1)} %gram_table.2.refs_0_, f32[1008,256]{1,0:T(8,128)S(1)} %gram_table.3.refs_1_, f32[2,128]{1,0:T(2,128)S(1)} %add.3.refs_2_, f32[2,128]{1,0:T(2,128)S(1)} %collective-permute-done.5.refs_3_, f32[2,128]{1,0:T(2,128)S(1)} %collective-permute-done.6.refs_4_, ...), custom_call_target="tpu_custom_call" | custom-call | tf_op jit(solution)/shard_map/analyse/pallas_call | solution.py:397
  (4 shorter events, 0.0 us)
Async XLA Ops:
  1.5 7.4 %collective-permute-start.2 = (f32[48,256]{1,0:T(8,128)S(1)}, f32[48,256]{1,0:T(8,128)S(1)}, u32[]{:S(2)}, u32[]{:S(2)}) collective-permute-start(f32[48,256]{1,0:T(8,128)S(1)} %prep.1), channel_id=1, source_target_pairs={{0,24},{8,16},{16,8},{24,0},{1,25},{9,17},{17,9},{25,1},{2,26},{10... | collective-permute-start | bytes 147464 | tf_op jit(solution)/shard_map/ppermute | solution.py:428
  5.5 4.1 %collective-permute-start.1 = (f32[48,256]{1,0:T(8,128)S(1)}, f32[48,256]{1,0:T(8,128)S(1)}, u32[]{:S(2)}, u32[]{:S(2)}) collective-permute-start(f32[48,256]{1,0:T(8,128)S(1)} %prep.1), channel_id=1, source_target_pairs={{0,16},{8,24},{16,0},{24,8},{1,17},{9,25},{17,1},{25,9},{2,18},{10... | collective-permute-start | bytes 147464 | tf_op jit(solution)/shard_map/ppermute | solution.py:428
  6.0 4.1 %collective-permute-start = (f32[48,256]{1,0:T(8,128)S(1)}, f32[48,256]{1,0:T(8,128)S(1)}, u32[]{:S(2)}, u32[]{:S(2)}) collective-permute-start(f32[48,256]{1,0:T(8,128)S(1)} %prep.1), channel_id=1, source_target_pairs={{0,8},{8,0},{16,24},{24,16},{1,9},{9,1},{17,25},{25,17},{2,10},{10... | collective-permute-start | bytes 147464 | tf_op jit(solution)/shard_map/ppermute | solution.py:428
  10.1 1.5 %collective-permute-start.3 = (f32[192,256]{1,0:T(8,128)S(1)}, f32[192,256]{1,0:T(8,128)S(1)}, u32[]{:S(2)}, u32[]{:S(2)}) collective-permute-start(f32[192,256]{1,0:T(8,128)S(1)} %pad_maximum_fusion.refs_0_), channel_id=1, source_target_pairs={{0,1},{1,0},{2,3},{3,2},{4,5},{5,4},{6,7},{7,6},{8,9},{9,8},{10,11... | collective-permute-start | bytes 589832 | tf_op jit(solution)/shard_map/ppermute | solution.py:428
  10.2 6.8 %collective-permute-start.4 = (f32[192,256]{1,0:T(8,128)S(1)}, f32[192,256]{1,0:T(8,128)S(1)}, u32[]{:S(2)}, u32[]{:S(2)}) collective-permute-start(f32[192,256]{1,0:T(8,128)S(1)} %pad_maximum_fusion.refs_0_), channel_id=1, source_target_pairs={{1,2},{2,1},{3,4},{4,3},{5,6},{6,5},{9,10},{10,9},{11,12},{12,11},... | collective-permute-start | bytes 589832 | tf_op jit(solution)/shard_map/ppermute | solution.py:434
  11.7 11.8 %collective-permute-start.7 = (f32[2,128]{1,0:T(2,128)S(1)}, f32[2,128]{1,0:T(2,128)S(1)}, u32[]{:S(2)}, u32[]{:S(2)}) collective-permute-start(f32[2,128]{1,0:T(2,128)S(1)} %add.3.refs_2_), channel_id=1, source_target_pairs={{0,6},{1,7},{2,4},{3,5},{4,2},{5,3},{6,0},{7,1},{8,14},{9,15},{10,... | collective-permute-start | bytes 3080 | tf_op jit(solution)/shard_map/ppermute | solution.py:428
  16.4 7.0 %collective-permute-start.6 = (f32[2,128]{1,0:T(2,128)S(1)}, f32[2,128]{1,0:T(2,128)S(1)}, u32[]{:S(2)}, u32[]{:S(2)}) collective-permute-start(f32[2,128]{1,0:T(2,128)S(1)} %add.3.refs_2_), channel_id=1, source_target_pairs={{0,4},{1,5},{2,6},{3,7},{4,0},{5,1},{6,2},{7,3},{8,12},{9,13},{10,... | collective-permute-start | bytes 3080 | tf_op jit(solution)/shard_map/ppermute | solution.py:428
  16.4 7.0 %collective-permute-start.5 = (f32[2,128]{1,0:T(2,128)S(1)}, f32[2,128]{1,0:T(2,128)S(1)}, u32[]{:S(2)}, u32[]{:S(2)}) collective-permute-start(f32[2,128]{1,0:T(2,128)S(1)} %add.3.refs_2_), channel_id=1, source_target_pairs={{0,2},{1,3},{2,0},{3,1},{4,6},{5,7},{6,4},{7,5},{8,10},{9,11},{10,... | collective-permute-start | bytes 3080 | tf_op jit(solution)/shard_map/ppermute | solution.py:428
